TPU v7x, 32 devices: a whole 2x2x4 slice. The times are simulated.
32 devices in a mesh: blk: 8 (over z, x), grid: 4 (over y, core).
Axes of the slice: x: 2, y: 2, z: 4, core: 2. Of those that a mesh axis runs over, the one named last changes fastest.
Arguments:
- patches: bfloat16 [4, 1024, 1024], P('grid', 'blk'), may hold values from -6 to 6
- stem_weight: bfloat16 [2, 1024, 768], replicated, may hold values from -0.125 to 0.125
- norm_gain: bfloat16 [768], replicated, may hold values from 0.25 to 1.75
- w_qkv: bfloat16 [768, 1280], replicated, may hold values from -0.21875 to 0.21875
- w_out: bfloat16 [768, 768], replicated, may hold values from -0.21875 to 0.21875
- per_head_scale: float32 [12], replicated, may hold values from 0.05 to 1, as said below
- positions: int32 [1024], replicated, may hold values from 0 to 1023, each once
- d_out: bfloat16 [4, 1024, 768], P('grid', 'blk'), may hold values from -48 to 48
Outputs:
- d_stem_weight: float32 [2, 1024, 768], P(None, None, ('blk', 'grid'))
- d_norm_gain: float32 [768], P(('blk', 'grid'))
- d_w_qkv: float32 [768, 1280], P(('blk', 'grid'))
- d_w_out: float32 [768, 768], P(None, ('blk', 'grid'))
Inputs may be any that keep to these rules, and one draw needn't show every extreme that they name: A permutation of the 1024 positions of a band. `per_head_scale`: positive.
All inputs are finite; a program needn't handle non-finite values.
Results may differ from a plain program's by a relative error of at most 0.015.
The roundings to bfloat16 on the way count: a program that leaves them out, or rounds other values in their place, can miss the bound.
Values may be sent and summed in bfloat16 or wider, within the bound.
A program may use at most 128 MiB of HBM per device.

v0:
```python
import jax
import jax.numpy as jnp
from jax import lax
from jax.sharding import PartitionSpec as P

QUERY_HEADS = 12
KEY_VALUE_HEADS = 4
HEAD_SIZE = 64
TC = 16


def shifted(x, axis, by):
    peers = lax.axis_size(axis)
    pairs = [(i, i + by) for i in range(peers) if 0 <= i + by < peers]
    return lax.ppermute(x, axis, pairs)


def passed_along(x, axis, by):
    peers = lax.axis_size(axis)
    return lax.ppermute(x, axis, [(i, (i + by) % peers) for i in range(peers)])


def row_norm(values):
    return values * lax.rsqrt(jnp.mean(values * values, axis=-1, keepdims=True) + 1e-05)


def head_norm(values):
    return values * lax.rsqrt(jnp.mean(values * values, axis=-1, keepdims=True) + 1e-06)


def shards(patches, stem_weight, norm_gain, w_qkv, w_out, per_head_scale, positions, d_out):
    tiles = patches[0]
    grad_out = d_out[0]
    token_rows = tiles.shape[0]
    group_factor = QUERY_HEADS // KEY_VALUE_HEADS
    query_span_width = QUERY_HEADS * HEAD_SIZE
    key_span_width = KEY_VALUE_HEADS * HEAD_SIZE
    arrived = shifted(tiles[:TC], "grid", -1)
    below = jnp.concatenate([tiles[TC:], arrived], axis=0)
    stem = jnp.dot(tiles, stem_weight[0], preferred_element_type=jnp.float32)
    stem = stem + jnp.dot(below, stem_weight[1], preferred_element_type=jnp.float32)
    token_f = lax.optimization_barrier(stem.astype(jnp.bfloat16)).astype(jnp.float32)
    gain_f = norm_gain.astype(jnp.float32)
    normed = row_norm(token_f)
    hidden = (normed * gain_f).astype(jnp.bfloat16)
    query_key_value = jnp.dot(hidden, w_qkv, preferred_element_type=jnp.float32)
    query = query_key_value[:, :query_span_width].reshape(token_rows, QUERY_HEADS, HEAD_SIZE)
    key = query_key_value[:, query_span_width : query_span_width + key_span_width].reshape(
        token_rows, KEY_VALUE_HEADS, HEAD_SIZE
    )
    query_normalized = head_norm(query).astype(jnp.bfloat16)
    key_n = head_norm(key).astype(jnp.bfloat16).reshape(token_rows, key_span_width)
    value = query_key_value[:, query_span_width + key_span_width :].astype(jnp.bfloat16)
    attention_gradient = jnp.dot(grad_out, w_out.T, preferred_element_type=jnp.float32).astype(
        jnp.bfloat16
    )
    kv_own = jnp.concatenate([key_n, value], axis=1)
    blk_count = lax.axis_size("blk")
    own_index = lax.axis_index("blk")
    blocks = [kv_own]
    for offset in range(1, 4):
        blocks.append(passed_along(kv_own, "blk", offset))
    causal_window = jnp.concatenate(blocks, axis=0)
    key_pos = jnp.concatenate(
        [
            lax.dynamic_slice_in_dim(
                positions, (own_index - offset) % blk_count * token_rows, token_rows
            )
            for offset in range(4)
        ]
    )
    query_pos = lax.dynamic_slice_in_dim(positions, own_index * token_rows, token_rows)
    visible = (key_pos[None, :] <= query_pos[:, None])[None]
    every_key = causal_window.shape[0]
    query_cube = query_normalized.reshape(token_rows, KEY_VALUE_HEADS, group_factor, HEAD_SIZE)
    gradient_cube = attention_gradient.reshape(token_rows, KEY_VALUE_HEADS, group_factor, HEAD_SIZE)
    key_cube = causal_window[:, :key_span_width].reshape(every_key, KEY_VALUE_HEADS, HEAD_SIZE)
    value_cube = causal_window[:, key_span_width:].reshape(every_key, KEY_VALUE_HEADS, HEAD_SIZE)
    score_scales = per_head_scale.reshape(KEY_VALUE_HEADS, group_factor)
    prob_list = []
    low_list = []
    attn_list = []
    for query_head_group in range(KEY_VALUE_HEADS):
        scale_col = score_scales[query_head_group][:, None, None]
        attention_scores = (
            jnp.einsum(
                "trd,sd->rts",
                query_cube[:, query_head_group],
                key_cube[:, query_head_group],
                preferred_element_type=jnp.float32,
            )
            * scale_col
        )
        attention_scores = jnp.where(visible, attention_scores, -1e30)
        top = jnp.max(attention_scores, axis=-1, keepdims=True)
        weights = jnp.where(visible, jnp.exp(attention_scores - top), 0.0)
        probs = weights / jnp.sum(weights, axis=-1, keepdims=True)
        probability_narrow = probs.astype(jnp.bfloat16)
        prob_list.append(probs)
        low_list.append(probability_narrow)
        attn_list.append(
            jnp.einsum(
                "rts,sd->trd",
                probability_narrow,
                value_cube[:, query_head_group],
                preferred_element_type=jnp.float32,
            )
        )
    attention_output = (
        jnp.stack(attn_list, axis=1).reshape(token_rows, query_span_width).astype(jnp.bfloat16)
    )
    out_term = jnp.dot(attention_output.T, grad_out, preferred_element_type=jnp.float32)
    d_w_out = lax.psum_scatter(out_term, ("blk", "grid"), scatter_dimension=1, tiled=True)
    dquery_list = []
    dkey_list = []
    dvalue_list = []
    for query_head_group in range(KEY_VALUE_HEADS):
        scale_col = score_scales[query_head_group][:, None, None]
        grad_group = gradient_cube[:, query_head_group]
        softmax_delta = jnp.sum(
            grad_group.astype(jnp.float32) * attn_list[query_head_group], axis=-1
        )
        probability_gradient = jnp.einsum(
            "trd,sd->rts",
            grad_group,
            value_cube[:, query_head_group],
            preferred_element_type=jnp.float32,
        )
        score_gradient = (
            scale_col
            * prob_list[query_head_group]
            * (probability_gradient - softmax_delta.T[:, :, None])
        ).astype(jnp.bfloat16)
        dquery_list.append(
            jnp.einsum(
                "rts,sd->trd",
                score_gradient,
                key_cube[:, query_head_group],
                preferred_element_type=jnp.float32,
            )
        )
        dkey_list.append(
            jnp.einsum(
                "rts,trd->sd",
                score_gradient,
                query_cube[:, query_head_group],
                preferred_element_type=jnp.float32,
            )
        )
        dvalue_list.append(
            jnp.einsum(
                "rts,trd->sd",
                low_list[query_head_group],
                grad_group,
                preferred_element_type=jnp.float32,
            )
        )
    query_gradient = jnp.stack(dquery_list, axis=1).reshape(token_rows, QUERY_HEADS, HEAD_SIZE)
    dkey_all = jnp.stack(dkey_list, axis=1).reshape(every_key, key_span_width)
    dvalue_all = jnp.stack(dvalue_list, axis=1).reshape(every_key, key_span_width)
    partial_terms = jnp.concatenate([dkey_all, dvalue_all], axis=1)
    pieces = [partial_terms[offset * token_rows : (offset + 1) * token_rows] for offset in range(4)]
    carried_state = pieces[3]
    for offset in (2, 1, 0):
        carried_state = passed_along(carried_state, "blk", -1) + pieces[offset]
    pull_query = jax.vjp(head_norm, query)[1]
    gather_key = jax.vjp(head_norm, key)[1]
    dq_full = pull_query(query_gradient)[0].reshape(token_rows, query_span_width)
    key_gradient_whole = gather_key(
        carried_state[:, :key_span_width].reshape(token_rows, KEY_VALUE_HEADS, HEAD_SIZE)
    )[0].reshape(token_rows, key_span_width)
    d_qkv = jnp.concatenate(
        [dq_full, key_gradient_whole, carried_state[:, key_span_width:]], axis=1
    ).astype(jnp.bfloat16)
    qkv_term = jnp.dot(hidden.T, d_qkv, preferred_element_type=jnp.float32)
    d_hidden = jnp.dot(d_qkv, w_qkv.T, preferred_element_type=jnp.float32)
    gain_term = jnp.sum(d_hidden * normed, axis=0)
    pull_tokens = jax.vjp(row_norm, token_f)[1]
    d_tokens = (grad_out.astype(jnp.float32) + pull_tokens(d_hidden * gain_f)[0]).astype(
        jnp.bfloat16
    )
    stem_term = jnp.stack(
        [
            jnp.dot(tiles.T, d_tokens, preferred_element_type=jnp.float32),
            jnp.dot(below.T, d_tokens, preferred_element_type=jnp.float32),
        ]
    )
    d_stem_weight, d_norm_gain, d_w_qkv = (
        lax.psum_scatter(stem_term, ("blk", "grid"), scatter_dimension=2, tiled=True),
        lax.psum_scatter(gain_term, ("blk", "grid"), scatter_dimension=0, tiled=True),
        lax.psum_scatter(qkv_term, ("blk", "grid"), scatter_dimension=0, tiled=True),
    )
    return (d_stem_weight, d_norm_gain, d_w_qkv, d_w_out)


def solution(mesh):
    placed = (P("grid", "blk", None), P(), P(), P(), P(), P(), P(), P("grid", "blk", None))
    return jax.shard_map(
        shards,
        mesh=mesh,
        in_specs=placed,
        out_specs=(
            P(None, None, ("blk", "grid")),
            P(("blk", "grid")),
            P(("blk", "grid"), None),
            P(None, ("blk", "grid")),
        ),
        check_vma=False,
    )
```

profile of v0, /device:TPU:0, one launch (start us, length us, event | category | flops | bytes accessed | tf_op | source)
XLA Modules:
  0.0 401.9 jit_solution(4561366616932660118)
XLA Ops:
  8.2 1.3 collective-permute-start
  10.5 1.9 fusion.6
  14.2 1.8 convolution_convert_fusion
  16.8 1.8 fusion.45
  20.9 3.0 collective-permute-start.1
  23.8 1.6 collective-permute-start.2
  25.4 2.6 collective-permute-start.3
  31.3 1.9 copy.95
  33.2 1.4 multiply_convert_fusion
  34.7 5.3 %collective-permute-done.3 = bf16[128,512]{1,0:T(8,128)(2,1)} collective-permute-done((bf16[128,512]{1,0:T(8,128)(2,1)}, bf16[128,512]{1,0:T(8,128)(2,1)}, u32[]{:S(2)}, u32[]{:S(2)}) %collective-permute-start.3) | collective-permute-done | bytes 131104 | tf_op jit(solution)/shard_map/ppermute | solution.py:20
  44.2 2.3 fusion.100
  46.5 2.3 fusion.99
  54.0 2.3 fusion.98
  59.3 2.3 fusion.97
  63.7 1.3 multiply_reduce_fusion.4
  65.0 1.9 fusion.70
  67.0 2.3 fusion.38
  78.6 1.2 copy.105
  79.9 1.2 convolution_bitcast_fusion.20
  85.0 3.3 collective-permute-done.4
  89.0 3.0 collective-permute-start.5
  93.0 1.9 copy.94
  94.9 2.6 collective-permute-done.5
  98.5 5.2 %collective-permute-start.6 = (f32[128,512]{1,0:T(8,128)S(1)}, f32[128,512]{1,0:T(8,128)S(1)}, u32[]{:S(2)}, u32[]{:S(2)}) collective-permute-start(f32[128,512]{1,0:T(8,128)S(1)} %fusion.63), channel_id=1, source_target_pairs={{0,28},{4,0},{8,4},{12,8},{16,12},{20,16},{24,20},{28,24},{1,29},{... | collective-permute-start | bytes 786440 | tf_op jit(solution)/shard_map/ppermute | solution.py:20
  103.7 1.4 fusion.52
  105.2 2.9 collective-permute-done.6
  111.1 2.7 fusion.73
  117.1 3.2 pad_maximum_fusion
  120.3 40.9 %all-reduce = f32[768]{0:T(1024)S(1)} all-reduce(f32[768]{0:T(1024)S(1)} %get-tuple-element.4), channel_id=3, replica_groups=mesh['blk'=8,'grid'=4] {'blk','grid'}, use_global_device_ids=true, to_apply=%region_20.21.clone | all-reduce | flops 768 | bytes 6144
  161.8 3.6 reduce-scatter.8.cloned.1.call-done
  165.5 109.7 %reduce-scatter.6.cloned.1.call-done = f32[24,1280]{1,0:T(8,128)} async-done(((f32[768,1280]{1,0:T(8,128)}), f32[24,1280]{1,0:T(8,128)}) %reduce-scatter.6.cloned.1.call-update) | async-done | bytes 122896 | tf_op jit(solution)/shard_map/reduce_scatter | solution.py:191
  275.2 120.2 %reduce-scatter.4.cloned.1.call-done = f32[2,1024,24]{1,2,0:T(8,128)} async-done(((f32[2,1024,768]{1,2,0:T(8,128)}), f32[2,1024,24]{1,2,0:T(8,128)}) %reduce-scatter.4.cloned.1.call-update) | async-done | bytes 196624 | tf_op jit(solution)/shard_map/reduce_scatter | solution.py:189
  (170 shorter events, 46.9 us)
Async XLA Ops:
  7.2 12.1 %copy-start = (bf16[768,1280]{1,0:T(8,128)(2,1)S(1)}, bf16[768,1280]{1,0:T(8,128)(2,1)}, u32[]{:S(2)}) copy-start(bf16[768,1280]{1,0:T(8,128)(2,1)} %param.11) | copy-start | bytes 5898244
  7.2 7.0 %copy-start.5 = (bf16[1,128,768]{2,1,0:T(8,128)(2,1)S(1)}, bf16[1,128,768]{2,1,0:T(8,128)(2,1)}, u32[]{:S(2)}) copy-start(bf16[1,128,768]{2,1,0:T(8,128)(2,1)} %param.15) | copy-start | bytes 589828
  7.2 8.8 %copy-start.29 = (f32[12]{0:T(128)S(1)}, f32[12]{0:T(128)}, u32[]{:S(2)}) copy-start(f32[12]{0:T(128)} %param.13) | copy-start | bytes 148
  7.2 9.4 %copy-start.32 = (bf16[768]{0:T(1024)(128)(2,1)S(1)}, bf16[768]{0:T(1024)(128)(2,1)}, u32[]{:S(2)}) copy-start(bf16[768]{0:T(1024)(128)(2,1)} %param.10) | copy-start | bytes 4612
  7.2 158.3 %reduce-scatter.8.cloned.1.call-start = ((), (), s32[]{:S(2)}) async-start(), calls=%async_computation.5 | async-start | bytes 2433024 | tf_op jit(solution)/shard_map/reduce_scatter | solution.py:113
  8.2 8.6 %collective-permute-start = (bf16[16,1024]{1,0:T(8,128)(2,1)S(1)}, bf16[16,1024]{1,0:T(8,128)(2,1)S(1)}, u32[]{:S(2)}, u32[]{:S(2)}) collective-permute-start(bf16[16,1024]{1,0:T(8,128)(2,1)S(1)} %slice_bitcast_fusion.73), channel_id=1, source_target_pairs={{1,0},{2,1},{3,2},{5,4},{6,5},{7,6},{9,8},{10,9},{11,10},{13,12},{... | collective-permute-start | bytes 98312 | tf_op jit(solution)/shard_map/ppermute | solution.py:15
  10.4 8.2 %copy-start.10 = (bf16[112,1024]{1,0:T(8,128)(2,1)}, bf16[112,1024]{1,0:T(8,128)(2,1)S(1)}, u32[]{:S(2)}) copy-start(bf16[112,1024]{1,0:T(8,128)(2,1)S(1)} %slice_bitcast_fusion) | copy-start | bytes 688132
  19.8 21.3 %copy-start.1 = (f32[128,1280]{1,0:T(8,128)}, f32[128,1280]{1,0:T(8,128)S(1)}, u32[]{:S(2)}) copy-start(f32[128,1280]{1,0:T(8,128)S(1)} %fusion.77) | copy-start | bytes 1966084
  19.9 8.1 %copy-start.18 = (bf16[128,256]{1,0:T(8,128)(2,1)}, bf16[128,256]{1,0:T(8,128)(2,1)S(1)}, u32[]{:S(2)}) copy-start(bf16[128,256]{1,0:T(8,128)(2,1)S(1)} %slice.325) | copy-start | bytes 196612
  20.0 7.9 %copy-start.27 = (f32[128,4]{0,1:T(4,128)}, f32[128,4]{0,1:T(4,128)S(1)}, u32[]{:S(2)}) copy-start(f32[128,4]{0,1:T(4,128)S(1)} %bitcast_reduce_fusion.1) | copy-start | bytes 6148
  20.2 7.8 %copy-start.17 = (bf16[128,256]{1,0:T(8,128)(2,1)}, bf16[128,256]{1,0:T(8,128)(2,1)S(1)}, u32[]{:S(2)}) copy-start(bf16[128,256]{1,0:T(8,128)(2,1)S(1)} %multiply_convert_fusion.1) | copy-start | bytes 196612
  20.9 13.8 %collective-permute-start.1 = (bf16[128,512]{1,0:T(8,128)(2,1)}, bf16[128,512]{1,0:T(8,128)(2,1)}, u32[]{:S(2)}, u32[]{:S(2)}) collective-permute-start(bf16[128,512]{1,0:T(8,128)(2,1)} %pad_maximum_fusion.13), channel_id=1, source_target_pairs={{0,4},{4,8},{8,12},{12,16},{16,20},{20,24},{24,28},{28,0},{1,5},{5... | collective-permute-start | bytes 393224 | tf_op jit(solution)/shard_map/ppermute | solution.py:20
  23.8 10.9 %collective-permute-start.2 = (bf16[128,512]{1,0:T(8,128)(2,1)}, bf16[128,512]{1,0:T(8,128)(2,1)}, u32[]{:S(2)}, u32[]{:S(2)}) collective-permute-start(bf16[128,512]{1,0:T(8,128)(2,1)} %pad_maximum_fusion.13), channel_id=1, source_target_pairs={{0,8},{4,12},{8,16},{12,20},{16,24},{20,28},{24,0},{28,4},{1,9},{5... | collective-permute-start | bytes 393224 | tf_op jit(solution)/shard_map/ppermute | solution.py:20
  25.4 14.6 %collective-permute-start.3 = (bf16[128,512]{1,0:T(8,128)(2,1)}, bf16[128,512]{1,0:T(8,128)(2,1)}, u32[]{:S(2)}, u32[]{:S(2)}) collective-permute-start(bf16[128,512]{1,0:T(8,128)(2,1)} %pad_maximum_fusion.13), channel_id=1, source_target_pairs={{0,12},{4,16},{8,20},{12,24},{16,28},{20,0},{24,4},{28,8},{1,13},{... | collective-permute-start | bytes 393224 | tf_op jit(solution)/shard_map/ppermute | solution.py:20
  31.3 12.8 %copy-start.37 = (f32[3]{0:T(128)S(1)}, f32[3]{0:T(128)}, u32[]{:S(2)}) copy-start(f32[3]{0:T(128)} %get-tuple-element.21) | copy-start | bytes 40
  31.3 15.2 %copy-start.36 = (f32[3]{0:T(128)S(1)}, f32[3]{0:T(128)}, u32[]{:S(2)}) copy-start(f32[3]{0:T(128)} %get-tuple-element.24) | copy-start | bytes 40
  43.0 16.3 %copy-start.9 = (bf16[512,256]{0,1:T(8,128)(2,1)}, bf16[512,256]{0,1:T(8,128)(2,1)S(1)}, u32[]{:S(2)}) copy-start(bf16[512,256]{0,1:T(8,128)(2,1)S(1)} %copy.81) | copy-start | bytes 786436
  46.5 7.5 %copy-start.35 = (f32[3]{0:T(128)S(1)}, f32[3]{0:T(128)}, u32[]{:S(2)}) copy-start(f32[3]{0:T(128)} %get-tuple-element.23) | copy-start | bytes 40
  51.4 7.9 %copy-start.39 = (f32[3]{0:T(128)S(1)}, f32[3]{0:T(128)}, u32[]{:S(2)}) copy-start(f32[3]{0:T(128)} %get-tuple-element.22) | copy-start | bytes 40
  63.7 3.3 copy-start.40
  66.9 208.2 %reduce-scatter.6.cloned.1.call-start = ((), (), s32[]{:S(2)}) async-start(), calls=%async_computation.4 | async-start | bytes 4055040 | tf_op jit(solution)/shard_map/reduce_scatter | solution.py:191
  67.0 3.4 copy-start.14
  79.9 8.4 %collective-permute-start.4 = (f32[128,512]{1,0:T(8,128)S(1)}, f32[128,512]{1,0:T(8,128)S(1)}, u32[]{:S(2)}, u32[]{:S(2)}) collective-permute-start(f32[128,512]{1,0:T(8,128)S(1)} %fusion.64), channel_id=1, source_target_pairs={{0,28},{4,0},{8,4},{12,8},{16,12},{20,16},{24,20},{28,24},{1,29},{... | collective-permute-start | bytes 786440 | tf_op jit(solution)/shard_map/ppermute | solution.py:20
  84.9 7.1 %copy-start.2 = (f32[128,4,3,64]{0,3,2,1:T(8,128)}, f32[128,4,3,64]{0,3,2,1:T(8,128)S(1)}, u32[]{:S(2)}) copy-start(f32[128,4,3,64]{0,3,2,1:T(8,128)S(1)} %pad_maximum_fusion.4) | copy-start | bytes 1179652
  89.0 8.5 %collective-permute-start.5 = (f32[128,512]{1,0:T(8,128)}, f32[128,512]{1,0:T(8,128)}, u32[]{:S(2)}, u32[]{:S(2)}) collective-permute-start(f32[128,512]{1,0:T(8,128)} %fusion.66), channel_id=1, source_target_pairs={{0,28},{4,0},{8,4},{12,8},{16,12},{20,16},{24,20},{28,24},{1,29},{... | collective-permute-start | bytes 786440 | tf_op jit(solution)/shard_map/ppermute | solution.py:20
  93.0 16.9 %copy-start.28 = (f32[128,4]{0,1:T(4,128)S(1)}, f32[128,4]{0,1:T(4,128)}, u32[]{:S(2)}) copy-start(f32[128,4]{0,1:T(4,128)} %copy-done.27) | copy-start | bytes 6148
  94.9 16.2 %copy-start.4 = (bf16[128,768]{1,0:T(8,128)(2,1)S(1)}, bf16[128,768]{1,0:T(8,128)(2,1)}, u32[]{:S(2)}) copy-start(bf16[128,768]{1,0:T(8,128)(2,1)} %copy-done.3) | copy-start | bytes 589828
  94.9 16.2 %copy-start.24 = (f32[768]{0:T(1024)S(1)}, f32[768]{0:T(1024)}, u32[]{:S(2)}) copy-start(f32[768]{0:T(1024)} %copy-done.23) | copy-start | bytes 9220
  94.9 16.2 %copy-start.31 = (f32[128]{0:T(128)S(1)}, f32[128]{0:T(128)}, u32[]{:S(2)}) copy-start(f32[128]{0:T(128)} %copy-done.30) | copy-start | bytes 1540
  98.5 9.6 %collective-permute-start.6 = (f32[128,512]{1,0:T(8,128)S(1)}, f32[128,512]{1,0:T(8,128)S(1)}, u32[]{:S(2)}, u32[]{:S(2)}) collective-permute-start(f32[128,512]{1,0:T(8,128)S(1)} %fusion.63), channel_id=1, source_target_pairs={{0,28},{4,0},{8,4},{12,8},{16,12},{20,16},{24,20},{28,24},{1,29},{... | collective-permute-start | bytes 786440 | tf_op jit(solution)/shard_map/ppermute | solution.py:20
  105.2 8.6 %copy-start.12 = (bf16[128,768]{1,0:T(8,128)(2,1)}, bf16[128,768]{1,0:T(8,128)(2,1)S(1)}, u32[]{:S(2)}) copy-start(bf16[128,768]{1,0:T(8,128)(2,1)S(1)} %fusion.52) | copy-start | bytes 589828
  113.8 281.5 %reduce-scatter.4.cloned.1.call-start = ((), (), s32[]{:S(2)}) async-start(), calls=%async_computation.3 | async-start | bytes 6488064 | tf_op jit(solution)/shard_map/reduce_scatter | solution.py:189
  (19 other events, 34.9 us)
Sparse Core Ops, SparseCore 0:
  67.1 98.3 reduce-scatter.7
  171.4 103.6 reduce-scatter.5
  281.4 113.8 reduce-scatter.3
where the time goes:
time: 403 us; the launch traced here: 402 us
  waiting for transfers between devices  248 us (62%)
  matrix products  44 us (11%)
  blocking collectives  40.9 us (10%)
  local copies, waits for them, and re-layouts  19.2 us (5%)
  other arithmetic  18.6 us (5%)
  starting transfers between devices  16.9 us (4%)
  between operations  14.6 us (4%)
    reduce_scatter x1, waiting for transfers between devices, shards(): lax.psum_scatter(stem_term, ('blk', 'grid'), scatter_dimension=2, tiled=T...  120 us
    reduce_scatter x1, waiting for transfers between devices, shards(): lax.psum_scatter(qkv_term, ('blk', 'grid'), scatter_dimension=0, tiled=True)  110 us
    unnamed x1, blocking collectives  40.9 us
    ppermute x6, starting transfers between devices, passed_along(): return lax.ppermute(x, axis, [(i, (i + by) % peers) for i in range(peers)])  15.4 us
    ppermute x6, waiting for transfers between devices, passed_along(): return lax.ppermute(x, axis, [(i, (i + by) % peers) for i in range(peers)])  14.1 us
    sub x4, matrix products, shards(): weights = jnp.where(visible, jnp.exp(attention_scores - top), 0.0)  9.17 us
  transfers between devices with their start and end apart: 10, of which 7 were waited for; matrix products, arithmetic and copies ran while one was open for 12% of the time, Pallas kernels for 0%

commit v1 on v0

--- a/solution.py
+++ b/solution.py
@@ -1,6 +1,10 @@
+from functools import partial
+
 import jax
 import jax.numpy as jnp
 from jax import lax
+from jax.experimental import pallas as pl
+from jax.experimental.pallas import tpu as pltpu
 from jax.sharding import PartitionSpec as P
 
 QUERY_HEADS = 12
@@ -26,6 +30,185 @@
 
 def head_norm(values):
     return values * lax.rsqrt(jnp.mean(values * values, axis=-1, keepdims=True) + 1e-06)
+
+
+def log2(n):
+    return n.bit_length() - 1
+
+
+def halving_orders(grid_bits, blk_bits):
+    y = list(range(grid_bits))
+    low = list(range(grid_bits, grid_bits + blk_bits))
+    rest = low[1:]
+    return [y + rest[:1] + rest[1:] + low[:1], low[:1] + y + rest, rest[:1] + low[:1] + y + rest[1:]]
+
+
+def chip_partner(bit, grid_bits, own_blk, own_grid):
+    if bit < grid_bits:
+        step = 2 << bit
+        mine = own_grid // step % 2
+        return {"blk": own_blk, "grid": own_grid + (1 - 2 * mine) * step}, mine
+    step = 1 << (bit - grid_bits)
+    mine = own_blk // step % 2
+    return {"blk": own_blk + (1 - 2 * mine) * step, "grid": own_grid}, mine
+
+
+def transposed_dot(a, b):
+    return lax.dot_general(a, b, (((0,), (0,)), ((), ())), preferred_element_type=jnp.float32)
+
+
+def scatter_kernel(nb, grid_bits, orders, widths, tok_ref, hid_ref, out_grad_ref, stem_ref, attn_ref, dqkv_ref, gain_ref, result_ref, *scratch):
+    scratch = list(scratch)
+    parts = len(widths)
+    first = [scratch.pop(0) for _ in range(parts)]
+    recv = [[scratch.pop(0) for _ in range(nb)] for _ in range(parts)]
+    send = [[None] + [scratch.pop(0) for _ in range(nb - 1)] for _ in range(parts)]
+    keep = [[scratch.pop(0) for _ in range(nb - 1)] for _ in range(parts)]
+    final, final_recv, send_sem, recv_sem, final_send, final_got = scratch
+    own_blk = lax.axis_index("blk")
+    own_grid = lax.axis_index("grid")
+    core = own_grid % 2
+    other_core = {"blk": own_blk, "grid": own_grid + 1 - 2 * core}
+    barrier = pltpu.get_barrier_semaphore()
+    for bit in range(nb):
+        pl.semaphore_signal(barrier, inc=1, device_id=chip_partner(bit, grid_bits, own_blk, own_grid)[0], device_id_type=pl.DeviceIdType.MESH)
+    pl.semaphore_signal(barrier, inc=1, device_id=other_core, device_id_type=pl.DeviceIdType.MESH)
+    pl.semaphore_wait(barrier, nb + 1)
+
+    def transfer(part, step, source):
+        partner, mine = chip_partner(orders[part][step], grid_bits, own_blk, own_grid)
+        copy = pltpu.make_async_remote_copy(
+            src_ref=source,
+            dst_ref=recv[part][step],
+            send_sem=send_sem.at[part, step],
+            recv_sem=recv_sem.at[part, step],
+            device_id=partner,
+            device_id_type=pl.DeviceIdType.MESH,
+        )
+        copy.start()
+        return copy
+
+    rows = final.shape[1] * 2
+    segments = [
+        [(tok_ref, stem_ref, 0, widths[0])],
+        [(tok_ref, stem_ref, widths[0], stem_ref.shape[1] - widths[0]), (out_grad_ref, attn_ref, 0, attn_ref.shape[1])],
+        [(hid_ref, dqkv_ref, 0, dqkv_ref.shape[1])],
+    ]
+    copies = [None] * parts
+    for part in (2, 1, 0):
+        at = 0
+        for left, right, start, width in segments[part]:
+            product = transposed_dot(left[...], right[:, start : start + width]).astype(jnp.bfloat16)
+            first[part][:, :, :, :, at : at + width] = product.reshape(first[part].shape[:4] + (width,))
+            at += width
+        if part == 2:
+            first[part][:, :, :, :, at:] = gain_ref[...].reshape(first[part].shape[:4] + (gain_ref.shape[1],))
+        mine = chip_partner(orders[part][0], grid_bits, own_blk, own_grid)[1]
+        copies[part] = transfer(part, 0, first[part].at[:, 1 - mine])
+
+    done = [None] * parts
+    for step in range(nb):
+        for part in (2, 1, 0):
+            copies[part].wait()
+            held = recv[part][step]
+            left_over = [b for b in range(nb) if b not in orders[part][:step]]
+            mine = chip_partner(orders[part][step], grid_bits, own_blk, own_grid)[1]
+            if step == 0:
+                inner = first[part].shape[2]
+
+                def total(i):
+                    return first[part][i // inner, mine, i % inner].astype(jnp.float32) + held[i // inner, i % inner].astype(jnp.float32)
+            else:
+                place = 1 << left_over.index(orders[part][step])
+
+                def total(i):
+                    return keep[part][step - 1][i // place * (2 * place) + mine * place + i % place] + held[i].astype(jnp.float32)
+
+            if step == nb - 1:
+                done[part] = total(0)
+                continue
+            left_over.remove(orders[part][step])
+            bit = orders[part][step + 1]
+            place_next = 1 << left_over.index(bit)
+            mine_next = chip_partner(bit, grid_bits, own_blk, own_grid)[1]
+            count = 1 << (nb - 1 - step)
+            for r in range(count // 2):
+                away = r // place_next * (2 * place_next) + (1 - mine_next) * place_next + r % place_next
+                send[part][step + 1][r] = total(away).astype(jnp.bfloat16)
+            copies[part] = transfer(part, step + 1, send[part][step + 1])
+            for r in range(count // 2):
+                here = r // place_next * (2 * place_next) + mine_next * place_next + r % place_next
+                keep[part][step][here] = total(here)
+    at = 0
+    half = rows // 2
+    for part in range(parts):
+        final[0, :, at : at + widths[part]] = done[part][:half]
+        final[1, :, at : at + widths[part]] = done[part][half:]
+        at += widths[part]
+    copy = pltpu.make_async_remote_copy(
+        src_ref=final.at[1 - core],
+        dst_ref=final_recv,
+        send_sem=final_send,
+        recv_sem=final_got,
+        device_id=other_core,
+        device_id_type=pl.DeviceIdType.MESH,
+    )
+    copy.start()
+    result_ref[core] = final[core]
+    copy.wait()
+    result_ref[1 - core] = final_recv[...]
+
+
+def scatter_all(tokens_grad, hidden, grad_out, stem_side, attn_side, qkv_side, gain):
+    blk_bits, grid_bits = log2(lax.axis_size("blk")), log2(lax.axis_size("grid")) - 1
+    nb = blk_bits + grid_bits
+    features = tokens_grad.shape[1]
+    rows = features >> nb
+    gain_tile = jnp.broadcast_to(gain.astype(jnp.bfloat16)[:, None], (features, 128))
+    stem_width = stem_side.shape[1]
+    widths = [stem_width * 3 // 4, stem_width // 4 + attn_side.shape[1], qkv_side.shape[1] + 128]
+    orders = halving_orders(grid_bits, blk_bits)
+    firsts, recvs, sends, keeps = [], [], [], []
+    for order, width in zip(orders, widths):
+        inner = 1 << order[0]
+        outer = (1 << nb) // (2 * inner)
+        firsts.append(pltpu.VMEM((outer, 2, inner, rows, width), jnp.bfloat16))
+        recvs.append(pltpu.VMEM((outer, inner, rows, width), jnp.bfloat16))
+        for step in range(1, nb):
+            shape = (1 << (nb - 1 - step), rows, width)
+            recvs.append(pltpu.VMEM(shape, jnp.bfloat16))
+            sends.append(pltpu.VMEM(shape, jnp.bfloat16))
+            keeps.append(pltpu.VMEM((1 << (nb - step), rows, width), jnp.float32))
+    total = sum(widths)
+    return pl.pallas_call(
+        partial(scatter_kernel, nb, grid_bits, orders, widths),
+        out_shape=jax.ShapeDtypeStruct((2, rows // 2, total), jnp.float32),
+        in_specs=[pl.BlockSpec(memory_space=pltpu.VMEM)] * 7,
+        out_specs=pl.BlockSpec(memory_space=pltpu.VMEM),
+        scratch_shapes=firsts
+        + recvs
+        + sends
+        + keeps
+        + [
+            pltpu.VMEM((2, rows // 2, total), jnp.float32),
+            pltpu.VMEM((rows // 2, total), jnp.float32),
+            pltpu.SemaphoreType.DMA((3, nb)),
+            pltpu.SemaphoreType.DMA((3, nb)),
+            pltpu.SemaphoreType.DMA,
+            pltpu.SemaphoreType.DMA,
+        ],
+        compiler_params=pltpu.CompilerParams(collective_id=0, has_side_effects=True, vmem_limit_bytes=60000000),
+    )(tokens_grad, hidden, grad_out, stem_side, attn_side, qkv_side, gain_tile)
+
+
+def across_cores(x):
+    peers = lax.axis_size("grid")
+    return lax.ppermute(x, "grid", [(i, i ^ 1) for i in range(peers)])
+
+
+def halved(x, core):
+    half = x.shape[1] // 2
+    return lax.dynamic_slice_in_dim(x, core * half, half, 1)
 
 
 def shards(patches, stem_weight, norm_gain, w_qkv, w_out, per_head_scale, positions, d_out):
@@ -37,6 +220,10 @@
     key_span_width = KEY_VALUE_HEADS * HEAD_SIZE
     arrived = shifted(tiles[:TC], "grid", -1)
     below = jnp.concatenate([tiles[TC:], arrived], axis=0)
+    core = lax.axis_index("grid") % 2
+    own_plane = jnp.where(core == 0, tiles, below)
+    stem_side = jnp.concatenate([own_plane, across_cores(jnp.where(core == 0, below, tiles))], axis=0)
+    grad_pair = jnp.concatenate([grad_out, across_cores(grad_out)], axis=0)
     stem = jnp.dot(tiles, stem_weight[0], preferred_element_type=jnp.float32)
     stem = stem + jnp.dot(below, stem_weight[1], preferred_element_type=jnp.float32)
     token_f = lax.optimization_barrier(stem.astype(jnp.bfloat16)).astype(jnp.float32)
@@ -109,8 +296,10 @@
     attention_output = (
         jnp.stack(attn_list, axis=1).reshape(token_rows, query_span_width).astype(jnp.bfloat16)
     )
-    out_term = jnp.dot(attention_output.T, grad_out, preferred_element_type=jnp.float32)
-    d_w_out = lax.psum_scatter(out_term, ("blk", "grid"), scatter_dimension=1, tiled=True)
+    attn_side = jnp.concatenate(
+        [halved(attention_output, core), across_cores(halved(attention_output, 1 - core))], axis=0
+    )
+    hidden_pair = jnp.concatenate([hidden, across_cores(hidden)], axis=0)
     dquery_list = []
     dkey_list = []
     dvalue_list = []
@@ -160,9 +349,9 @@
     dvalue_all = jnp.stack(dvalue_list, axis=1).reshape(every_key, key_span_width)
     partial_terms = jnp.concatenate([dkey_all, dvalue_all], axis=1)
     pieces = [partial_terms[offset * token_rows : (offset + 1) * token_rows] for offset in range(4)]
-    carried_state = pieces[3]
-    for offset in (2, 1, 0):
-        carried_state = passed_along(carried_state, "blk", -1) + pieces[offset]
+    carried_state = pieces[0]
+    for offset in (1, 2, 3):
+        carried_state = carried_state + passed_along(pieces[offset], "blk", -offset)
     pull_query = jax.vjp(head_norm, query)[1]
     gather_key = jax.vjp(head_norm, key)[1]
     dq_full = pull_query(query_gradient)[0].reshape(token_rows, query_span_width)
@@ -172,24 +361,36 @@
     d_qkv = jnp.concatenate(
         [dq_full, key_gradient_whole, carried_state[:, key_span_width:]], axis=1
     ).astype(jnp.bfloat16)
-    qkv_term = jnp.dot(hidden.T, d_qkv, preferred_element_type=jnp.float32)
+    qkv_side = jnp.concatenate([halved(d_qkv, core), across_cores(halved(d_qkv, 1 - core))], axis=0)
     d_hidden = jnp.dot(d_qkv, w_qkv.T, preferred_element_type=jnp.float32)
     gain_term = jnp.sum(d_hidden * normed, axis=0)
     pull_tokens = jax.vjp(row_norm, token_f)[1]
     d_tokens = (grad_out.astype(jnp.float32) + pull_tokens(d_hidden * gain_f)[0]).astype(
         jnp.bfloat16
     )
+    tokens_pair = jnp.concatenate([d_tokens, across_cores(d_tokens)], axis=0)
+    chips = blk_count * lax.axis_size("grid") // 2
+    if (d_tokens.shape[1] // chips) % 16 == 0:
+        parts = scatter_all(tokens_pair, hidden_pair, grad_pair, stem_side, attn_side, qkv_side, gain_term)
+        stem_width, attn_width, qkv_width = stem_side.shape[1], attn_side.shape[1], qkv_side.shape[1]
+        d_stem_weight = parts[:, :, :stem_width].transpose(0, 2, 1)
+        d_w_out = parts[:, :, stem_width : stem_width + attn_width].transpose(0, 2, 1).reshape(2 * attn_width, -1)
+        start = stem_width + attn_width
+        d_w_qkv = jnp.concatenate([parts[0, :, start : start + qkv_width], parts[1, :, start : start + qkv_width]], axis=1)
+        d_norm_gain = parts[0, :, start + qkv_width] + parts[1, :, start + qkv_width]
+        return (d_stem_weight, d_norm_gain, d_w_qkv, d_w_out)
     stem_term = jnp.stack(
         [
             jnp.dot(tiles.T, d_tokens, preferred_element_type=jnp.float32),
             jnp.dot(below.T, d_tokens, preferred_element_type=jnp.float32),
         ]
     )
-    d_stem_weight, d_norm_gain, d_w_qkv = (
-        lax.psum_scatter(stem_term, ("blk", "grid"), scatter_dimension=2, tiled=True),
-        lax.psum_scatter(gain_term, ("blk", "grid"), scatter_dimension=0, tiled=True),
-        lax.psum_scatter(qkv_term, ("blk", "grid"), scatter_dimension=0, tiled=True),
-    )
+    qkv_term = jnp.dot(hidden.T, d_qkv, preferred_element_type=jnp.float32)
+    out_term = jnp.dot(attention_output.T, grad_out, preferred_element_type=jnp.float32)
+    d_stem_weight = lax.psum_scatter(stem_term, ("blk", "grid"), scatter_dimension=2, tiled=True)
+    d_norm_gain = lax.psum_scatter(gain_term, ("blk", "grid"), scatter_dimension=0, tiled=True)
+    d_w_qkv = lax.psum_scatter(qkv_term, ("blk", "grid"), scatter_dimension=0, tiled=True)
+    d_w_out = lax.psum_scatter(out_term, ("blk", "grid"), scatter_dimension=1, tiled=True)
     return (d_stem_weight, d_norm_gain, d_w_qkv, d_w_out)
 
 

time: 403 us -> 171 us (0.42)
  waiting for transfers between devices: 248 us -> 14.2 us
  Pallas kernels: 0 us -> 53.5 us
  blocking collectives: 40.9 us -> 0 us
  between operations: 14.6 us -> 1.37 us
  other arithmetic: 18.6 us -> 31.5 us
  matrix products: 44 us -> 33.6 us
  starting transfers between devices: 16.9 us -> 12.6 us
    reduce_scatter x3 -> x0, waiting for transfers between devices: 233 us -> none  [the longest x1 120 us: shards(): lax.psum_scatter(stem_term, ('blk', 'grid'), scatter_dimension=2, tiled=T...]
    pallas_call x0 -> x1, Pallas kernels: none -> 53.5 us  [scatter_all(): pl.pallas_call(partial(scatter_kernel, nb, grid_bits, orders, widths), ou...]
    unnamed x1 -> x0, blocking collectives: 40.9 us -> none
    concatenate x0 -> x8, other arithmetic: none -> 9.15 us  [the longest x1 1.79 us: shards(): hidden_pair = jnp.concatenate([hidden, across_cores(hidden)], axis=0)]
    ppermute x6, starting transfers between devices: 15.4 us -> 8.95 us  [passed_along(): return lax.ppermute(x, axis, [(i, (i + by) % peers) for i in range(peers)])]
    dot_general x4 -> x0, matrix products: 5.8 us -> none  [the longest x1 2.71 us: shards(): qkv_term = jnp.dot(hidden.T, d_qkv, preferred_element_type=jnp.float32)]
    dot_general x4, matrix products: 5.45 us -> 1.19 us  [shards(): jnp.einsum('trd,sd->rts', grad_group, value_cube[:, query_head_group], pr...]
    dot_general x4, matrix products: 4.95 us -> 0.79 us  [shards(): jnp.einsum('rts,sd->trd', score_gradient, key_cube[:, query_head_group],...]
  transfers between devices with their start and end apart: 10 -> 13, of which waited for: 7 -> 3; matrix products, arithmetic and copies ran while one was open for 12% -> 45% of each run, Pallas kernels for 0% -> 0%
where the time goes in v1:
time: 171 us; the launch traced here: 169 us
  Pallas kernels  53.5 us (31%)
  matrix products  33.6 us (20%)
  other arithmetic  31.5 us (18%)
  local copies, waits for them, and re-layouts  22.6 us (13%)
  waiting for transfers between devices  14.2 us (8%)
  starting transfers between devices  12.6 us (7%)
    pallas_call x1, Pallas kernels, scatter_all(): pl.pallas_call(partial(scatter_kernel, nb, grid_bits, orders, widths), ou...  53.5 us
    ppermute x6, waiting for transfers between devices, passed_along(): return lax.ppermute(x, axis, [(i, (i + by) % peers) for i in range(peers)])  14.2 us
    sub x4, matrix products, shards(): weights = jnp.where(visible, jnp.exp(attention_scores - top), 0.0)  9.76 us
    ppermute x6, starting transfers between devices, passed_along(): return lax.ppermute(x, axis, [(i, (i + by) % peers) for i in range(peers)])  8.95 us
    dot_general x4, matrix products, shards(): jnp.einsum('rts,trd->sd', low_list[query_head_group], grad_group, preferr...  5.23 us
    dot_general x4, matrix products, shards(): jnp.einsum('rts,sd->trd', probability_narrow, value_cube[:, query_head_gr...  4.65 us
    unnamed x89, local copies, waits for them, and re-layouts  4.55 us
    convert_element_type x4, other arithmetic, shards(): probability_narrow = probs.astype(jnp.bfloat16)  3.84 us
  transfers between devices with their start and end apart: 13, of which 3 were waited for; matrix products, arithmetic and copies ran while one was open for 45% of the time, Pallas kernels for 0%

profile of v1, /device:TPU:0, one launch (start us, length us, event | category | flops | bytes accessed | tf_op | source)
XLA Modules:
  0.0 169.4 jit_solution(2031321633328819319)
XLA Ops:
  0.7 1.5 slice_bitcast_fusion.77
  4.7 1.6 slice_bitcast_fusion
  6.3 2.7 %fusion.6 = f32[128,768]{1,0:T(8,128)} fusion(bf16[2,1024,768]{2,1,0:T(8,128)(2,1)} %param.9, bf16[1,128,1024]{2,1,0:T(8,128)(2,1)} %param.8), kind=kOutput, calls=%fused_computation.6 | convolution fusion | flops 201326592 | bytes 2228224 | tf_op jit(solution)/shard_map/dot_general | solution.py:227
  11.9 2.0 %fusion.45 = bf16[128,768]{1,0:T(8,128)(2,1)S(1)} fusion(f32[128,768]{1,0:T(8,128)} %fusion.6, bf16[2,1024,768]{2,1,0:T(8,128)(2,1)} %param.9, bf16[16,1024]{1,0:T(8,128)(2,1)} %collective-permute-done, bf16[112,1024]{1,0:T(8,128)(2,1)} %slice_bitcast_fusion), kind=kOutput, calls=%fused_computation.57 | convolution fusion | flops 202047488 | bytes 2424832 | tf_op jit(solution)/shard_map/dot_general | solution.py:228
  15.9 1.4 fusion.91
  18.8 3.0 %collective-permute-start.1 = (bf16[128,512]{1,0:T(8,128)(2,1)}, bf16[128,512]{1,0:T(8,128)(2,1)}, u32[]{:S(2)}, u32[]{:S(2)}) collective-permute-start(bf16[128,512]{1,0:T(8,128)(2,1)} %pad_maximum_fusion.14), channel_id=1, source_target_pairs={{0,4},{4,8},{8,12},{12,16},{16,20},{20,24},{24,28},{28,0},{1,5},{5... | collective-permute-start | bytes 393224 | tf_op jit(solution)/shard_map/ppermute | solution.py:24
  21.8 1.6 collective-permute-start.2
  23.4 2.6 %collective-permute-start.3 = (bf16[128,512]{1,0:T(8,128)(2,1)}, bf16[128,512]{1,0:T(8,128)(2,1)}, u32[]{:S(2)}, u32[]{:S(2)}) collective-permute-start(bf16[128,512]{1,0:T(8,128)(2,1)} %pad_maximum_fusion.14), channel_id=1, source_target_pairs={{0,12},{4,16},{8,20},{12,24},{16,28},{20,0},{24,4},{28,8},{1,13},{... | collective-permute-start | bytes 393224 | tf_op jit(solution)/shard_map/ppermute | solution.py:24
  27.8 2.0 %bitcast_select_fusion.1 = (bf16[128,1024]{1,0:T(8,128)(2,1)}, bf16[128,1024]{1,0:T(8,128)(2,1)}) fusion(bf16[1,128,1024]{2,1,0:T(8,128)(2,1)} %param.8, pred[]{:T(512)S(6)} %eq.10, bf16[16,1024]{1,0:T(8,128)(2,1)} %collective-permute-done, bf16[112,1024]{1,0:T(8,128)(2,1)} %slice_bitcast_fusion), kind=kLoop, calls=%fused_computation.121 | loop fusion | flops 786432 | bytes 1048577 | tf_op jit(solution)/shard_map/jit(_where)/select_n | solution.py:224
  29.8 1.4 multiply_convert_fusion
  31.7 5.6 %collective-permute-done.3 = bf16[128,512]{1,0:T(8,128)(2,1)} collective-permute-done((bf16[128,512]{1,0:T(8,128)(2,1)}, bf16[128,512]{1,0:T(8,128)(2,1)}, u32[]{:S(2)}, u32[]{:S(2)}) %collective-permute-start.3) | collective-permute-done | bytes 131104 | tf_op jit(solution)/shard_map/ppermute | solution.py:24
  40.4 2.3 %fusion.90 = (f32[3,128]{1,0:T(4,128)S(1)}, f32[3,128,512]{1,2,0:T(8,128)}) fusion(f32[3]{0:T(128)S(1)} %copy-done.40, pred[128,512]{0,1:T(8,128)(4,1)} %broadcast_compare_fusion, bf16[512,4,64]{0,2,1:T(8,128)(2,1)S(1)} %bitcast.342, bf16[128,4,3,64]{0,3,2,1:T(8,128)(2,1)} %multiply_convert_fusion), kind=kOutput, calls=%fused_computation.199 | convolution fusion | flops 26149376 | bytes 1034240 | tf_op jit(solution)/shard_map/sub | solution.py:283
  42.7 2.3 %fusion.89 = (f32[3,128]{1,0:T(4,128)S(1)}, f32[3,128,512]{1,2,0:T(8,128)}) fusion(f32[3]{0:T(128)} %get-tuple-element.35, pred[128,512]{0,1:T(8,128)(4,1)} %broadcast_compare_fusion, bf16[512,4,64]{0,2,1:T(8,128)(2,1)S(1)} %bitcast.343, bf16[128,4,3,64]{0,3,2,1:T(8,128)(2,1)} %multiply_convert_fusion), kind=kOutput, calls=%fused_computation.198 | convolution fusion | flops 26149376 | bytes 1034240 | tf_op jit(solution)/shard_map/sub | solution.py:283
  49.9 2.3 %fusion.88 = (f32[3,128]{1,0:T(4,128)S(1)}, f32[3,128,512]{1,2,0:T(8,128)}) fusion(f32[3]{0:T(128)} %get-tuple-element.34, pred[128,512]{0,1:T(8,128)(4,1)} %broadcast_compare_fusion, bf16[512,4,64]{0,2,1:T(8,128)(2,1)S(1)} %bitcast.344, bf16[128,4,3,64]{0,3,2,1:T(8,128)(2,1)} %multiply_convert_fusion), kind=kOutput, calls=%fused_computation.197 | convolution fusion | flops 26149376 | bytes 1034240 | tf_op jit(solution)/shard_map/sub | solution.py:283
  54.3 1.7 %convolution_bitcast_fusion.4 = f32[512,1,64]{0,2,1:T(8,128)} fusion(bf16[3,128,512]{1,2,0:T(8,128)(2,1)S(1)} %fusion.61, bf16[128,4,3,64]{0,3,2,1:T(8,128)(2,1)} %bitcast.358), kind=kOutput, calls=%fused_computation.59 | convolution fusion | flops 25165824 | bytes 573440 | tf_op jit(solution)/shard_map/rts,trd->sd/dot_general | solution.py:340
  56.0 2.9 %fusion.87 = (f32[3,128]{1,0:T(4,128)}, f32[3,128,512]{1,2,0:T(8,128)}) fusion(f32[3]{0:T(128)} %get-tuple-element.32, pred[128,512]{0,1:T(8,128)(4,1)} %broadcast_compare_fusion, bf16[512,4,64]{0,2,1:T(8,128)(2,1)S(1)} %bitcast.345, bf16[128,4,3,64]{0,3,2,1:T(8,128)(2,1)} %multiply_convert_fusion), kind=kOutput, calls=%fused_computation.196 | convolution fusion | flops 26149376 | bytes 1034240 | tf_op jit(solution)/shard_map/sub | solution.py:283
  60.2 1.7 %convolution_bitcast_fusion.7 = f32[512,1,64]{0,2,1:T(8,128)} fusion(bf16[3,128,512]{1,2,0:T(8,128)(2,1)S(1)} %fusion.58, bf16[128,4,3,64]{0,3,2,1:T(8,128)(2,1)} %bitcast.359), kind=kOutput, calls=%fused_computation.62 | convolution fusion | flops 25165824 | bytes 573440 | tf_op jit(solution)/shard_map/rts,trd->sd/dot_general | solution.py:340
  61.9 2.1 %multiply_reduce_fusion.4 = (f32[128,3]{0,1:T(4,128)S(1)}, f32[128,3]{0,1:T(4,128)S(1)}, f32[128,3]{0,1:T(4,128)S(1)}, f32[128,3]{0,1:T(4,128)S(1)}, bf16[128,1,...) fusion(bf16[128,4,3,64]{0,3,2,1:T(8,128)(2,1)} %bitcast.360, ...), kind=kOutput, calls=%fused_computation.142 | convolution fusion | flops 25557504 | bytes 1153024 | tf_op jit(solution)/shard_map/rts,sd->trd/dot_general | solution.py:289
  72.1 1.9 %pad_maximum_fusion.2 = f32[512,4,64]{0,2,1:T(8,128)} fusion(f32[512,1,64]{0,2,1:T(8,128)} %convolution_bitcast_fusion.4, f32[512,1,64]{0,2,1:T(8,128)} %convolution_bitcast_fusion.5, f32[512,1,64]{0,2,1:T(8,128)S(1)} %copy-done.18, f32[512,1,64]{0,2,1:T(8,128)} %convolution_bitcast_fusion.7), kind=kLoop, calls=%fused_computation.83 | loop fusion | flops 393216 | bytes 1048576 | tf_op jit(solution)/shard_map/stack | solution.py:349
  75.2 1.9 %pad_maximum_fusion.1 = f32[512,4,64]{0,2,1:T(8,128)} fusion(f32[512,1,64]{0,2,1:T(8,128)} %convolution_bitcast_fusion.8, f32[512,1,64]{0,2,1:T(8,128)} %convolution_bitcast_fusion.9, f32[512,1,64]{0,2,1:T(8,128)} %convolution_bitcast_fusion.10, f32[512,1,64]{0,2,1:T(8,128)S(1)} %copy-done.19), kind=kLoop, calls=%fused_computation.82 | loop fusion | flops 393216 | bytes 1048576 | tf_op jit(solution)/shard_map/stack | solution.py:348
  77.1 2.0 %copy.73 = f32[512,256]{1,0:T(8,128)} copy(f32[512,256]{0,1:T(8,128)} %bitcast.337) | data formatting | bytes 1048576 | tf_op jit(solution)/shard_map/reshape | solution.py:348
  79.1 2.0 %fusion.67 = (f32[128,512]{1,0:T(8,128)}, f32[128,512]{1,0:T(8,128)}, f32[128,512]{1,0:T(8,128)}) fusion(f32[512,256]{1,0:T(8,128)} %copy.73, f32[512,256]{1,0:T(8,128)S(1)} %copy.74), kind=kLoop, calls=%fused_computation.117 | loop fusion | flops 196608 | bytes 1835008 | tf_op jit(solution)/shard_map/concatenate | solution.py:350
  81.1 1.6 collective-permute-start.5
  82.7 2.0 %fusion.52 = bf16[128,768]{1,0:T(8,128)(2,1)} fusion(f32[128,768]{1,0:T(8,128)} %copy.64, f32[128,768]{1,0:T(8,128)} %copy.62, f32[128,768]{1,0:T(8,128)} %copy.63, f32[128,1280]{1,0:T(8,128)S(1)} %fusion.91), kind=kLoop, calls=%fused_computation.89 | loop fusion | flops 491520 | bytes 1769472 | tf_op jit(solution)/shard_map/convert.8
  86.0 1.7 %pad_maximum_fusion.7.out_grad_ref = bf16[256,768]{1,0:T(8,128)(2,1)} fusion(bf16[128,768]{1,0:T(8,128)(2,1)} %collective-permute-done.9, bf16[128,768]{1,0:T(8,128)(2,1)S(1)} %bitcast.339), kind=kLoop, calls=%fused_computation.97 | loop fusion | flops 786432 | bytes 786432 | tf_op jit(solution)/shard_map/concatenate | solution.py:226
  87.7 1.8 %pad_maximum_fusion.6.hid_ref = bf16[256,768]{1,0:T(8,128)(2,1)} fusion(bf16[128,768]{1,0:T(8,128)(2,1)} %collective-permute-done.8, bf16[128,768]{1,0:T(8,128)(2,1)} %fusion.50), kind=kLoop, calls=%fused_computation.96 | loop fusion | flops 786432 | bytes 786432 | tf_op jit(solution)/shard_map/concatenate | solution.py:302
  90.2 3.6 %collective-permute-done.5 = f32[128,512]{1,0:T(8,128)} collective-permute-done((f32[128,512]{1,0:T(8,128)}, f32[128,512]{1,0:T(8,128)}, u32[]{:S(2)}, u32[]{:S(2)}) %collective-permute-start.5) | collective-permute-done | bytes 262176 | tf_op jit(solution)/shard_map/ppermute | solution.py:24
  93.8 5.0 %collective-permute-done.6 = f32[128,512]{1,0:T(8,128)S(1)} collective-permute-done((f32[128,512]{1,0:T(8,128)}, f32[128,512]{1,0:T(8,128)S(1)}, u32[]{:S(2)}, u32[]{:S(2)}) %collective-permute-start.6) | collective-permute-done | bytes 262176 | tf_op jit(solution)/shard_map/ppermute | solution.py:24
  102.9 1.9 %fusion.51 = (bf16[768]{0:T(1024)(128)(2,1)S(1)}, f32[128]{0:T(128)S(1)}, f32[128,768]{1,0:T(8,128)S(1)}) fusion(bf16[128,768]{1,0:T(8,128)(2,1)S(1)} %copy-done.5, f32[128]{0:T(128)S(1)} %copy-done.33, f32[768]{0:T(1024)S(1)} %copy-done.25, bf16[768,1280]{1,0:T(8,128)(2,1)S(1)} %copy-done, bf16[128,256]{1,0:T(8,128)(2,1)S(1)} %slice.356, ...), kind=kOutput, calls=%fused_computation.88 | convolution fusion | flops 253328512 | bytes 2889216 | tf_op jit(solution)/shard_map/dot_general | solution.py:365
  105.6 1.8 %pad_maximum_fusion.3.stem_ref = bf16[256,1024]{1,0:T(8,128)(2,1)} fusion(bf16[128,1024]{1,0:T(8,128)(2,1)} %collective-permute-done.10, bf16[128,1024]{1,0:T(8,128)(2,1)S(1)} %copy-done.9), kind=kLoop, calls=%fused_computation.84 | loop fusion | flops 1048576 | bytes 1048576 | tf_op jit(solution)/shard_map/concatenate | solution.py:225
  109.8 53.5 %shard_map.111 = f32[2,24,2176]{2,1,0:T(8,128)} custom-call(bf16[256,768]{1,0:T(8,128)(2,1)} %pad_maximum_fusion.5.tok_ref, bf16[256,768]{1,0:T(8,128)(2,1)} %pad_maximum_fusion.6.hid_ref, bf16[256,768]{1,0:T(8,128)(2,1)} %pad_maximum_fusion.7.out_grad_ref, bf16[256,1024]{1,0:T(8,128)(2,1)} %pad_maximum_fusion.3.stem_ref, ...), custom_call_target="tpu_custom_call" | custom-call | tf_op jit(solution)/shard_map/pallas_call | solution.py:183
  164.2 1.6 slice_bitcast_fusion.1
  (189 shorter events, 45.3 us)
Async XLA Ops:
  0.6 15.3 %copy-start = (bf16[768,1280]{1,0:T(8,128)(2,1)S(1)}, bf16[768,1280]{1,0:T(8,128)(2,1)}, u32[]{:S(2)}) copy-start(bf16[768,1280]{1,0:T(8,128)(2,1)} %param.11) | copy-start | bytes 5898244
  0.6 8.3 %copy-start.2 = (bf16[1,128,768]{2,1,0:T(8,128)(2,1)S(1)}, bf16[1,128,768]{2,1,0:T(8,128)(2,1)}, u32[]{:S(2)}) copy-start(bf16[1,128,768]{2,1,0:T(8,128)(2,1)} %param.15) | copy-start | bytes 589828
  0.7 8.3 %copy-start.7 = (bf16[768,768]{1,0:T(8,128)(2,1)S(1)}, bf16[768,768]{1,0:T(8,128)(2,1)}, u32[]{:S(2)}) copy-start(bf16[768,768]{1,0:T(8,128)(2,1)} %param.12) | copy-start | bytes 3538948
  2.2 9.7 %collective-permute-start = (bf16[16,1024]{1,0:T(8,128)(2,1)}, bf16[16,1024]{1,0:T(8,128)(2,1)}, u32[]{:S(2)}, u32[]{:S(2)}) collective-permute-start(bf16[16,1024]{1,0:T(8,128)(2,1)} %slice_bitcast_fusion.77), channel_id=1, source_target_pairs={{1,0},{2,1},{3,2},{5,4},{6,5},{7,6},{9,8},{10,9},{11,10},{13,12},{... | collective-permute-start | bytes 98312 | tf_op jit(solution)/shard_map/ppermute | solution.py:19
  3.5 82.2 %collective-permute-start.9 = (bf16[128,768]{1,0:T(8,128)(2,1)}, bf16[128,768]{1,0:T(8,128)(2,1)}, u32[]{:S(2)}, u32[]{:S(2)}) collective-permute-start(bf16[128,768]{1,0:T(8,128)(2,1)} %bitcast.338), channel_id=1, source_target_pairs={{0,1},{1,0},{2,3},{3,2},{4,5},{5,4},{6,7},{7,6},{8,9},{9,8},{10,11... | collective-permute-start | bytes 589832 | tf_op jit(solution)/shard_map/ppermute | solution.py:206
  18.1 7.9 %copy-start.8 = (f32[128,256]{1,0:T(8,128)}, f32[128,256]{1,0:T(8,128)S(1)}, u32[]{:S(2)}) copy-start(f32[128,256]{1,0:T(8,128)S(1)} %copy.48) | copy-start | bytes 393220
  18.8 12.4 %collective-permute-start.1 = (bf16[128,512]{1,0:T(8,128)(2,1)}, bf16[128,512]{1,0:T(8,128)(2,1)}, u32[]{:S(2)}, u32[]{:S(2)}) collective-permute-start(bf16[128,512]{1,0:T(8,128)(2,1)} %pad_maximum_fusion.14), channel_id=1, source_target_pairs={{0,4},{4,8},{8,12},{12,16},{16,20},{20,24},{24,28},{28,0},{1,5},{5... | collective-permute-start | bytes 393224 | tf_op jit(solution)/shard_map/ppermute | solution.py:24
  21.8 9.9 %collective-permute-start.2 = (bf16[128,512]{1,0:T(8,128)(2,1)}, bf16[128,512]{1,0:T(8,128)(2,1)}, u32[]{:S(2)}, u32[]{:S(2)}) collective-permute-start(bf16[128,512]{1,0:T(8,128)(2,1)} %pad_maximum_fusion.14), channel_id=1, source_target_pairs={{0,8},{4,12},{8,16},{12,20},{16,24},{20,28},{24,0},{28,4},{1,9},{5... | collective-permute-start | bytes 393224 | tf_op jit(solution)/shard_map/ppermute | solution.py:24
  23.4 14.0 %collective-permute-start.3 = (bf16[128,512]{1,0:T(8,128)(2,1)}, bf16[128,512]{1,0:T(8,128)(2,1)}, u32[]{:S(2)}, u32[]{:S(2)}) collective-permute-start(bf16[128,512]{1,0:T(8,128)(2,1)} %pad_maximum_fusion.14), channel_id=1, source_target_pairs={{0,12},{4,16},{8,20},{12,24},{16,28},{20,0},{24,4},{28,8},{1,13},{... | collective-permute-start | bytes 393224 | tf_op jit(solution)/shard_map/ppermute | solution.py:24
  26.0 61.7 %collective-permute-start.8 = (bf16[128,768]{1,0:T(8,128)(2,1)}, bf16[128,768]{1,0:T(8,128)(2,1)}, u32[]{:S(2)}, u32[]{:S(2)}) collective-permute-start(bf16[128,768]{1,0:T(8,128)(2,1)} %fusion.50), channel_id=1, source_target_pairs={{0,1},{1,0},{2,3},{3,2},{4,5},{5,4},{6,7},{7,6},{8,9},{9,8},{10,11... | collective-permute-start | bytes 589832 | tf_op jit(solution)/shard_map/ppermute | solution.py:206
  29.8 10.6 %copy-start.40 = (f32[3]{0:T(128)S(1)}, f32[3]{0:T(128)}, u32[]{:S(2)}) copy-start(f32[3]{0:T(128)} %get-tuple-element.33) | copy-start | bytes 40
  31.2 74.4 %collective-permute-start.10 = (bf16[128,1024]{1,0:T(8,128)(2,1)}, bf16[128,1024]{1,0:T(8,128)(2,1)}, u32[]{:S(2)}, u32[]{:S(2)}) collective-permute-start(bf16[128,1024]{1,0:T(8,128)(2,1)} %get-tuple-element.14), channel_id=1, source_target_pairs={{0,1},{1,0},{2,3},{3,2},{4,5},{5,4},{6,7},{7,6},{8,9},{9,8},{10,11... | collective-permute-start | bytes 786440 | tf_op jit(solution)/shard_map/ppermute | solution.py:206
  58.9 5.1 %copy-start.11 = (bf16[128,768]{0,1:T(8,128)(2,1)S(1)}, bf16[128,768]{0,1:T(8,128)(2,1)}, u32[]{:S(2)}) copy-start(bf16[128,768]{0,1:T(8,128)(2,1)} %copy.53) | copy-start | bytes 589828
  58.9 5.1 %copy-start.16 = (f32[3,128,512]{1,2,0:T(8,128)S(1)}, f32[3,128,512]{1,2,0:T(8,128)}, u32[]{:S(2)}) copy-start(f32[3,128,512]{1,2,0:T(8,128)} %get-tuple-element.37) | copy-start | bytes 2359300
  58.9 5.1 %copy-start.31 = (f32[3,128]{1,0:T(4,128)S(1)}, f32[3,128]{1,0:T(4,128)}, u32[]{:S(2)}) copy-start(f32[3,128]{1,0:T(4,128)} %get-tuple-element.36) | copy-start | bytes 4612
  58.9 5.1 %copy-start.42 = (f32[3]{0:T(128)S(1)}, f32[3]{0:T(128)}, u32[]{:S(2)}) copy-start(f32[3]{0:T(128)} %get-tuple-element.32) | copy-start | bytes 40
  79.1 5.6 %copy-start.20 = (bf16[128,1,3,64]{0,3,2,1:T(8,128)(2,1)S(1)}, bf16[128,1,3,64]{0,3,2,1:T(8,128)(2,1)}, u32[]{:S(2)}) copy-start(bf16[128,1,3,64]{0,3,2,1:T(8,128)(2,1)} %get-tuple-element.23) | copy-start | bytes 147460
  79.1 5.6 %copy-start.21 = (bf16[128,1,3,64]{0,3,2,1:T(8,128)(2,1)S(1)}, bf16[128,1,3,64]{0,3,2,1:T(8,128)(2,1)}, u32[]{:S(2)}) copy-start(bf16[128,1,3,64]{0,3,2,1:T(8,128)(2,1)} %get-tuple-element.24) | copy-start | bytes 147460
  79.1 5.6 %copy-start.22 = (bf16[128,1,3,64]{0,3,2,1:T(8,128)(2,1)S(1)}, bf16[128,1,3,64]{0,3,2,1:T(8,128)(2,1)}, u32[]{:S(2)}) copy-start(bf16[128,1,3,64]{0,3,2,1:T(8,128)(2,1)} %get-tuple-element.25) | copy-start | bytes 147460
  79.1 5.6 %copy-start.23 = (bf16[128,1,3,64]{0,3,2,1:T(8,128)(2,1)S(1)}, bf16[128,1,3,64]{0,3,2,1:T(8,128)(2,1)}, u32[]{:S(2)}) copy-start(bf16[128,1,3,64]{0,3,2,1:T(8,128)(2,1)} %get-tuple-element.26) | copy-start | bytes 147460
  79.1 6.8 %copy-start.3 = (bf16[1,128,768]{2,1,0:T(8,128)(2,1)S(1)}, bf16[1,128,768]{2,1,0:T(8,128)(2,1)}, u32[]{:S(2)}) copy-start(bf16[1,128,768]{2,1,0:T(8,128)(2,1)} %param.15) | copy-start | bytes 589828
  81.1 9.1 %collective-permute-start.4 = (f32[128,512]{1,0:T(8,128)}, f32[128,512]{1,0:T(8,128)}, u32[]{:S(2)}, u32[]{:S(2)}) collective-permute-start(f32[128,512]{1,0:T(8,128)} %get-tuple-element.10), channel_id=1, source_target_pairs={{0,28},{4,0},{8,4},{12,8},{16,12},{20,16},{24,20},{28,24},{1,29},{... | collective-permute-start | bytes 786440 | tf_op jit(solution)/shard_map/ppermute | solution.py:24
  81.1 12.7 %collective-permute-start.5 = (f32[128,512]{1,0:T(8,128)}, f32[128,512]{1,0:T(8,128)}, u32[]{:S(2)}, u32[]{:S(2)}) collective-permute-start(f32[128,512]{1,0:T(8,128)} %get-tuple-element.12), channel_id=1, source_target_pairs={{0,24},{4,28},{8,0},{12,4},{16,8},{20,12},{24,16},{28,20},{1,25},{... | collective-permute-start | bytes 786440 | tf_op jit(solution)/shard_map/ppermute | solution.py:24
  85.7 13.1 %copy-start.1 = (f32[512,256]{1,0:T(8,128)S(1)}, f32[512,256]{1,0:T(8,128)}, u32[]{:S(2)}) copy-start(f32[512,256]{1,0:T(8,128)} %copy.73) | copy-start | bytes 1572868
  85.7 13.0 %collective-permute-start.6 = (f32[128,512]{1,0:T(8,128)}, f32[128,512]{1,0:T(8,128)S(1)}, u32[]{:S(2)}, u32[]{:S(2)}) collective-permute-start(f32[128,512]{1,0:T(8,128)} %get-tuple-element.11), channel_id=1, source_target_pairs={{0,20},{4,24},{8,28},{12,0},{16,4},{20,8},{24,12},{28,16},{1,21},{... | collective-permute-start | bytes 786440 | tf_op jit(solution)/shard_map/ppermute | solution.py:24
  87.7 13.0 %copy-start.27 = (f32[128,4]{0,1:T(4,128)S(1)}, f32[128,4]{0,1:T(4,128)}, u32[]{:S(2)}) copy-start(f32[128,4]{0,1:T(4,128)} %copy-done.26) | copy-start | bytes 6148
  87.7 1.8 %collective-permute-start.11 = (bf16[128,384]{1,0:T(8,128)(2,1)}, bf16[128,384]{1,0:T(8,128)(2,1)S(1)}, u32[]{:S(2)}, u32[]{:S(2)}) collective-permute-start(bf16[128,384]{1,0:T(8,128)(2,1)} %copy.98), channel_id=1, source_target_pairs={{0,1},{1,0},{2,3},{3,2},{4,5},{5,4},{6,7},{7,6},{8,9},{9,8},{10,11... | collective-permute-start | bytes 294920 | tf_op jit(solution)/shard_map/ppermute | solution.py:206
  90.2 12.6 %copy-start.5 = (bf16[128,768]{1,0:T(8,128)(2,1)S(1)}, bf16[128,768]{1,0:T(8,128)(2,1)}, u32[]{:S(2)}) copy-start(bf16[128,768]{1,0:T(8,128)(2,1)} %copy-done.4) | copy-start | bytes 589828
  90.2 12.7 %copy-start.25 = (f32[768]{0:T(1024)S(1)}, f32[768]{0:T(1024)}, u32[]{:S(2)}) copy-start(f32[768]{0:T(1024)} %copy-done.24) | copy-start | bytes 9220
  90.2 12.7 %copy-start.33 = (f32[128]{0:T(128)S(1)}, f32[128]{0:T(128)}, u32[]{:S(2)}) copy-start(f32[128]{0:T(128)} %copy-done.32) | copy-start | bytes 1540
  104.8 2.6 %collective-permute-start.12 = (bf16[128,640]{1,0:T(8,128)(2,1)S(1)}, bf16[128,640]{1,0:T(8,128)(2,1)S(1)}, u32[]{:S(2)}, u32[]{:S(2)}) collective-permute-start(bf16[128,640]{1,0:T(8,128)(2,1)S(1)} %get-tuple-element.20), channel_id=1, source_target_pairs={{0,1},{1,0},{2,3},{3,2},{4,5},{5,4},{6,7},{7,6},{8,9},{9,8},{10,11... | collective-permute-start | bytes 491528 | tf_op jit(solution)/shard_map/ppermute | solution.py:206
  105.1 3.1 %collective-permute-start.7 = (bf16[128,768]{1,0:T(8,128)(2,1)S(1)}, bf16[128,768]{1,0:T(8,128)(2,1)S(1)}, u32[]{:S(2)}, u32[]{:S(2)}) collective-permute-start(bf16[128,768]{1,0:T(8,128)(2,1)S(1)} %fusion.54), channel_id=1, source_target_pairs={{0,1},{1,0},{2,3},{3,2},{4,5},{5,4},{6,7},{7,6},{8,9},{9,8},{10,11... | collective-permute-start | bytes 589832 | tf_op jit(solution)/shard_map/ppermute | solution.py:206
  (24 other events, 51.7 us)

commit v2 on v0

--- a/solution.py
+++ b/solution.py
@@ -1,6 +1,10 @@
+from functools import partial
+
 import jax
 import jax.numpy as jnp
 from jax import lax
+from jax.experimental import pallas as pl
+from jax.experimental.pallas import tpu as pltpu
 from jax.sharding import PartitionSpec as P
 
 QUERY_HEADS = 12
@@ -28,9 +32,385 @@
     return values * lax.rsqrt(jnp.mean(values * values, axis=-1, keepdims=True) + 1e-06)
 
 
+def log2(n):
+    return n.bit_length() - 1
+
+
+def halving_orders(grid_bits, blk_bits):
+    y = list(range(grid_bits))
+    low = list(range(grid_bits, grid_bits + blk_bits))
+    rest = low[1:]
+    return [y + rest[:1] + rest[1:] + low[:1], low[:1] + y + rest, rest[:1] + low[:1] + y + rest[1:]]
+
+
+def chip_partner(bit, grid_bits, own_blk, own_grid):
+    if bit < grid_bits:
+        step = 2 << bit
+        mine = own_grid // step % 2
+        return {"blk": own_blk, "grid": own_grid + (1 - 2 * mine) * step}, mine
+    step = 1 << (bit - grid_bits)
+    mine = own_blk // step % 2
+    return {"blk": own_blk + (1 - 2 * mine) * step, "grid": own_grid}, mine
+
+
+def transposed_dot(a, b):
+    return lax.dot_general(a, b, (((0,), (0,)), ((), ())), preferred_element_type=jnp.float32)
+
+
+def rowwise_dot(a, b):
+    return lax.dot_general(a, b, (((1,), (1,)), ((), ())), preferred_element_type=jnp.float32)
+
+
+def plain_dot(a, b):
+    return jnp.dot(a, b, preferred_element_type=jnp.float32)
+
+
+def half_sums(x):
+    low = lax.broadcasted_iota(jnp.int32, x.shape, 1) < HEAD_SIZE
+    first = jnp.sum(jnp.where(low, x, 0.0), axis=1, keepdims=True)
+    second = jnp.sum(jnp.where(low, 0.0, x), axis=1, keepdims=True)
+    return jnp.where(low, first, second)
+
+
+def layer_kernel(plan, *refs):
+    nb, grid_bits, orders, widths, offsets = plan
+    (scale_ref, tiles_ref, grad_ref, stem_hbm, gain_ref, wqkv_hbm, wout_hbm, pos_ref, result_ref) = refs[:9]
+    scratch = list(refs[9:])
+    parts = len(widths)
+    first = [scratch.pop(0) for _ in range(parts)]
+    recv = [[scratch.pop(0) for _ in range(nb)] for _ in range(parts)]
+    send = [[None] + [scratch.pop(0) for _ in range(nb - 1)] for _ in range(parts)]
+    keep = [[scratch.pop(0) for _ in range(nb - 1)] for _ in range(parts)]
+    (final, final_recv, stem_w, wqkv, wout, image, grad_pair, hidden_pair, attn_pair, dqkv_pair, token_pair,
+     kv, dkv_out, dkv_own, dkv_in, normed_ref, inv_ref, qk_ref, heads_inv, qn, da, attn, dq, dqkv,
+     load_sem, pair_send, pair_got, halo_send, halo_got, kv_send, kv_got, dkv_send, dkv_got, send_sem, recv_sem) = scratch
+    tok, width = grad_ref.shape
+    halo = image.shape[0] - 2 * tok
+    span = kv.shape[2] // 2
+    group = QUERY_HEADS // KEY_VALUE_HEADS
+    own_blk = lax.axis_index("blk")
+    own_grid = lax.axis_index("grid")
+    blk_count = lax.axis_size("blk")
+    grid_count = lax.axis_size("grid")
+    core = own_grid % 2
+    other_core = {"blk": own_blk, "grid": own_grid + 1 - 2 * core}
+    above = {"blk": own_blk, "grid": (own_grid + grid_count - 1) % grid_count}
+    under = {"blk": own_blk, "grid": (own_grid + 1) % grid_count}
+
+    def along(offset):
+        return {"blk": (own_blk + offset + blk_count) % blk_count, "grid": own_grid}
+
+    loads = [
+        pltpu.make_async_copy(stem_hbm, stem_w, load_sem.at[0]),
+        pltpu.make_async_copy(wqkv_hbm, wqkv, load_sem.at[1]),
+        pltpu.make_async_copy(wout_hbm, wout, load_sem.at[2]),
+    ]
+    for load in loads:
+        load.start()
+
+    barrier = pltpu.get_barrier_semaphore()
+    peers = [chip_partner(bit, grid_bits, own_blk, own_grid)[0] for bit in range(nb)]
+    peers += [other_core, above, under] + [along(j) for j in (1, 2, 3, -1, -2, -3)]
+    for peer in peers:
+        pl.semaphore_signal(barrier, inc=1, device_id=peer, device_id_type=pl.DeviceIdType.MESH)
+    pl.semaphore_wait(barrier, len(peers))
+
+    def push(source, target, sems, got, device):
+        copy = pltpu.make_async_remote_copy(
+            src_ref=source, dst_ref=target, send_sem=sems, recv_sem=got, device_id=device, device_id_type=pl.DeviceIdType.MESH
+        )
+        copy.start()
+        return copy
+
+    def pair(which, source, target):
+        return push(source, target, pair_send.at[which], pair_got.at[which], other_core)
+
+    own_rows = pl.ds(pl.multiple_of(core * tok, tok), tok)
+    tiles_copy = pair(0, tiles_ref, image.at[own_rows])
+    halo_copy = push(tiles_ref.at[:halo], image.at[2 * tok :], halo_send, halo_got, above)
+    grad_copy = pair(1, grad_ref, grad_pair.at[core])
+    image[own_rows] = tiles_ref[...]
+    grad_pair[core] = grad_ref[...]
+
+    loads[0].wait()
+    stem = plain_dot(tiles_ref[...], stem_w[0])
+    tiles_copy.wait()
+    halo_copy.wait()
+
+    @pl.when(own_grid == grid_count - 1)
+    def _():
+        image[2 * tok :] = jnp.zeros((halo, image.shape[1]), image.dtype)
+
+    below = image[pl.ds(pl.multiple_of(core * tok + halo, halo), tok)]
+    stem = stem + plain_dot(below, stem_w[1])
+    token_f = stem.astype(jnp.bfloat16).astype(jnp.float32)
+    inv = lax.rsqrt(jnp.sum(token_f * token_f, axis=1, keepdims=True) / width + 1e-05)
+    normed = token_f * inv
+    normed_ref[...] = normed
+    inv_ref[...] = jnp.broadcast_to(inv, inv_ref.shape)
+    gain_f = gain_ref[...].astype(jnp.float32)
+    hidden = (normed * gain_f).astype(jnp.bfloat16)
+    hidden_pair[core] = hidden
+    hidden_copy = pair(2, hidden_pair.at[core], hidden_pair.at[core])
+    loads[1].wait()
+    key_start = QUERY_HEADS * HEAD_SIZE
+    value_start = key_start + span
+
+    def normalize(x):
+        scale = lax.rsqrt(half_sums(x * x) / HEAD_SIZE + 1e-06)
+        return scale, (x * scale).astype(jnp.bfloat16)
+
+    keys = plain_dot(hidden, wqkv[:, key_start:])
+    for at in range(0, span, 128):
+        x = keys[:, at : at + 128]
+        heads_inv[:, key_start + at : key_start + at + 128], kv[0, :, at : at + 128] = normalize(x)
+    kv[0, :, span:] = keys[:, span:].astype(jnp.bfloat16)
+    qk_ref[:, key_start:] = keys[:, :span]
+    kv_copies = [push(kv.at[0], kv.at[j], kv_send.at[j], kv_got.at[j], along(j)) for j in (1, 2, 3)]
+    queries = plain_dot(hidden, wqkv[:, :key_start])
+    qk_ref[:, :key_start] = queries
+    for at in range(0, key_start, 128):
+        heads_inv[:, at : at + 128], qn[:, at : at + 128] = normalize(queries[:, at : at + 128])
+    loads[2].wait()
+    da[...] = rowwise_dot(grad_ref[...], wout[...]).astype(jnp.bfloat16)
+
+    query_pos = pos_ref[pl.ds(own_blk, 1), :]
+    seen = []
+    for j in range(4):
+        key_pos = pos_ref[pl.ds((own_blk + blk_count - j) % blk_count, 1), :]
+        column = jnp.broadcast_to(key_pos, (tok, tok)).T
+        seen.append(column <= query_pos)
+    visible = jnp.concatenate([jnp.where(x, 1.0, 0.0) for x in seen], axis=0) > 0.5
+    for copy in kv_copies:
+        copy.wait()
+
+    for g in range(KEY_VALUE_HEADS):
+        lanes = slice(g * HEAD_SIZE, (g + 1) * HEAD_SIZE)
+        value_lanes = slice(span + g * HEAD_SIZE, span + (g + 1) * HEAD_SIZE)
+        keys_g = kv[:, :, lanes].reshape(4 * tok, HEAD_SIZE)
+        values_g = kv[:, :, value_lanes].reshape(4 * tok, HEAD_SIZE)
+        heads = [slice((g * group + i) * HEAD_SIZE, (g * group + i + 1) * HEAD_SIZE) for i in range(group)]
+        queries_g = jnp.concatenate([qn[:, h] for h in heads], axis=0)
+        grads_g = jnp.concatenate([da[:, h] for h in heads], axis=0)
+        scores = rowwise_dot(keys_g, queries_g)
+        dprobs = rowwise_dot(values_g, grads_g)
+        probs, low = [], []
+        for i in range(group):
+            s = jnp.where(visible, scores[:, i * tok : (i + 1) * tok] * scale_ref[g * group + i], -1e30)
+            weights = jnp.where(visible, jnp.exp(s - jnp.max(s, axis=0, keepdims=True)), 0.0)
+            p = weights * (1.0 / jnp.sum(weights, axis=0, keepdims=True))
+            probs.append(p)
+            low.append(p.astype(jnp.bfloat16))
+        low_g = jnp.concatenate(low, axis=1)
+        attn_t = transposed_dot(values_g, low_g)
+        delta = jnp.sum(grads_g.astype(jnp.float32).T * attn_t, axis=0, keepdims=True)
+        ds = []
+        for i in range(group):
+            cols = slice(i * tok, (i + 1) * tok)
+            ds.append((scale_ref[g * group + i] * probs[i] * (dprobs[:, cols] - delta[:, cols])).astype(jnp.bfloat16))
+        ds_g = jnp.concatenate(ds, axis=1)
+        dq_g = transposed_dot(keys_g, ds_g).T
+        attn_g = attn_t.T
+        for i in range(group):
+            attn[:, heads[i]] = attn_g[i * tok : (i + 1) * tok].astype(jnp.bfloat16)
+            dq[:, heads[i]] = dq_g[i * tok : (i + 1) * tok]
+        dkeys = plain_dot(ds_g, queries_g).reshape(4, tok, HEAD_SIZE)
+        dvalues = plain_dot(low_g, grads_g).reshape(4, tok, HEAD_SIZE)
+        dkv_own[:, lanes] = dkeys[0]
+        dkv_own[:, value_lanes] = dvalues[0]
+        for j in (1, 2, 3):
+            dkv_out[j - 1, :, lanes] = dkeys[j].astype(jnp.bfloat16)
+            dkv_out[j - 1, :, value_lanes] = dvalues[j].astype(jnp.bfloat16)
+    dkv_copies = [push(dkv_out.at[j - 1], dkv_in.at[j - 1], dkv_send.at[j - 1], dkv_got.at[j - 1], along(-j)) for j in (3, 2, 1)]
+    half_attn = attn.shape[1] // 2
+    attn_copy = pair(3, attn.at[:, pl.ds(pl.multiple_of((1 - core) * half_attn, 128), half_attn)], attn_pair.at[core])
+    attn_pair[core] = attn[:, pl.ds(pl.multiple_of(core * half_attn, 128), half_attn)]
+
+    def pull(at, g):
+        scale = heads_inv[:, at : at + 128]
+        x = qk_ref[:, at : at + 128] * scale
+        return (scale * (g - x * (half_sums(g * x) / HEAD_SIZE))).astype(jnp.bfloat16)
+
+    for at in range(0, key_start, 128):
+        dqkv[:, at : at + 128] = pull(at, dq[:, at : at + 128])
+
+    copies = [None] * parts
+    steps = [0] * parts
+    done = [None] * parts
+
+    def transfer(part, source):
+        partner = chip_partner(orders[part][steps[part]], grid_bits, own_blk, own_grid)[0]
+        copies[part] = push(source, recv[part][steps[part]], send_sem.at[part, steps[part]], recv_sem.at[part, steps[part]], partner)
+
+    def begin(members, left, right, extra=None):
+        product = transposed_dot(left.reshape(2 * tok, width), right).astype(jnp.bfloat16)
+        if extra is not None:
+            product = jnp.concatenate([product, extra], axis=1)
+        at = 0
+        for part in members:
+            first[part][...] = product[:, at : at + widths[part]].reshape(first[part].shape)
+            at += widths[part]
+            mine = chip_partner(orders[part][0], grid_bits, own_blk, own_grid)[1]
+            transfer(part, first[part].at[:, 1 - mine])
+
+    def advance(part):
+        step = steps[part]
+        order = orders[part]
+        copies[part].wait()
+        held = recv[part][step]
+        mine = chip_partner(order[step], grid_bits, own_blk, own_grid)[1]
+        left_over = [b for b in range(nb) if b not in order[:step]]
+        inner = first[part].shape[2]
+
+        def total(i):
+            if step == 0:
+                return first[part][i // inner, mine, i % inner].astype(jnp.float32) + held[i // inner, i % inner].astype(jnp.float32)
+            return keep[part][step - 1][i] + held[i].astype(jnp.float32)
+
+        steps[part] = step + 1
+        if step == nb - 1:
+            value = total(0)
+            half = value.shape[0] // 2
+            final[0, :, offsets[part] : offsets[part] + widths[part]] = value[:half]
+            final[1, :, offsets[part] : offsets[part] + widths[part]] = value[half:]
+            return
+        left_over.remove(order[step])
+        place_next = 1 << left_over.index(order[step + 1])
+        mine_next = chip_partner(order[step + 1], grid_bits, own_blk, own_grid)[1]
+        count = 1 << (nb - 2 - step)
+        for r in range(count):
+            away = r // place_next * (2 * place_next) + (1 - mine_next) * place_next + r % place_next
+            send[part][step + 1][r] = total(away).astype(jnp.bfloat16)
+        transfer(part, send[part][step + 1])
+        for r in range(count):
+            here = r // place_next * (2 * place_next) + mine_next * place_next + r % place_next
+            keep[part][step][r] = total(here)
+
+    attn_parts, qkv_parts, stem_parts = (0, 1, 2), (3, 4, 5), (6, 7, 8)
+    attn_copy.wait()
+    grad_copy.wait()
+    begin(attn_parts, grad_pair[...], attn_pair[...].reshape(2 * tok, half_attn))
+
+    for copy in dkv_copies:
+        copy.wait()
+    total_kv = dkv_own[...]
+    for j in range(3):
+        total_kv = total_kv + dkv_in[j].astype(jnp.float32)
+    for at in range(0, span, 128):
+        dqkv[:, key_start + at : key_start + at + 128] = pull(key_start + at, total_kv[:, at : at + 128])
+    dqkv[:, value_start:] = total_kv[:, span:].astype(jnp.bfloat16)
+    half_qkv = dqkv.shape[1] // 2
+    dqkv_copy = pair(4, dqkv.at[:, pl.ds(pl.multiple_of((1 - core) * half_qkv, 128), half_qkv)], dqkv_pair.at[core])
+    dqkv_pair[core] = dqkv[:, pl.ds(pl.multiple_of(core * half_qkv, 128), half_qkv)]
+    d_hidden = rowwise_dot(dqkv[...], wqkv[...])
+    normed = normed_ref[...]
+    flow = d_hidden * gain_f
+    inner_mean = jnp.sum(flow * normed, axis=1, keepdims=True) / width
+    d_tokens = grad_ref[...].astype(jnp.float32) + inv_ref[:, :1] * (flow - normed * inner_mean)
+    token_pair[core] = d_tokens.astype(jnp.bfloat16)
+    token_copy = pair(5, token_pair.at[core], token_pair.at[core])
+    gain_term = jnp.sum(d_hidden * normed, axis=0, keepdims=True)
+    gain_tile = jnp.broadcast_to(gain_term, (128, width)).T.astype(jnp.bfloat16)
+    hidden_copy.wait()
+    dqkv_copy.wait()
+    begin(qkv_parts, hidden_pair[...], dqkv_pair[...].reshape(2 * tok, half_qkv))
+    token_copy.wait()
+    begin(stem_parts, token_pair[...], image[pl.ds(pl.multiple_of(core * halo, halo), 2 * tok)], gain_tile)
+    for _ in range(nb):
+        for part in range(parts):
+            advance(part)
+    copy = pair(6, final.at[1 - core], final_recv)
+    result_ref[core] = final[core]
+    copy.wait()
+    result_ref[1 - core] = final_recv[...]
+
+
+def whole_layer(tiles, grad_out, stem_weight, norm_gain, w_qkv, w_out, per_head_scale, positions):
+    blk_bits, grid_bits = log2(lax.axis_size("blk")), log2(lax.axis_size("grid")) - 1
+    nb = blk_bits + grid_bits
+    tok, width = grad_out.shape
+    pin = tiles.shape[1]
+    qd, span = QUERY_HEADS * HEAD_SIZE, KEY_VALUE_HEADS * HEAD_SIZE
+    rows = width >> nb
+    half_qkv = w_qkv.shape[1] // 2
+    part_widths = []
+    for amount in (qd // 2, half_qkv, pin + 128):
+        piece = (amount // 3 + 127) // 128 * 128
+        part_widths += [piece, piece, amount - 2 * piece]
+    offsets = [sum(part_widths[:i]) for i in range(9)]
+    orders = halving_orders(grid_bits, blk_bits) * 3
+    firsts, recvs, sends, keeps = [], [], [], []
+    for order, w in zip(orders, part_widths):
+        inner = 1 << order[0]
+        outer = (1 << nb) // (2 * inner)
+        firsts.append(pltpu.VMEM((outer, 2, inner, rows, w), jnp.bfloat16))
+        recvs.append(pltpu.VMEM((outer, inner, rows, w), jnp.bfloat16))
+        for step in range(1, nb):
+            shape = (1 << (nb - 1 - step), rows, w)
+            recvs.append(pltpu.VMEM(shape, jnp.bfloat16))
+            sends.append(pltpu.VMEM(shape, jnp.bfloat16))
+            keeps.append(pltpu.VMEM(shape, jnp.float32))
+    total = sum(part_widths)
+    bf, f32 = jnp.bfloat16, jnp.float32
+    buffers = [
+        ((2, rows // 2, total), f32),
+        ((rows // 2, total), f32),
+        (stem_weight.shape, bf),
+        (w_qkv.shape, bf),
+        (w_out.shape, bf),
+        ((2 * tok + TC, pin), bf),
+        ((2, tok, width), bf),
+        ((2, tok, width), bf),
+        ((2, tok, qd // 2), bf),
+        ((2, tok, half_qkv), bf),
+        ((2, tok, width), bf),
+        ((4, tok, 2 * span), bf),
+        ((3, tok, 2 * span), bf),
+        ((tok, 2 * span), f32),
+        ((3, tok, 2 * span), bf),
+        ((tok, width), f32),
+        ((tok, 128), f32),
+        ((tok, qd + span), f32),
+        ((tok, qd + span), f32),
+        ((tok, qd), bf),
+        ((tok, qd), bf),
+        ((tok, qd), bf),
+        ((tok, qd), f32),
+        ((tok, w_qkv.shape[1]), bf),
+    ]
+    dma = pltpu.SemaphoreType.DMA
+    vmem = pl.BlockSpec(memory_space=pltpu.VMEM)
+    hbm = pl.BlockSpec(memory_space=pl.ANY)
+    return part_widths, pl.pallas_call(
+        partial(layer_kernel, (nb, grid_bits, orders, part_widths, offsets)),
+        out_shape=jax.ShapeDtypeStruct((2, rows // 2, total), f32),
+        in_specs=[pl.BlockSpec(memory_space=pltpu.SMEM), vmem, vmem, hbm, vmem, hbm, hbm, vmem],
+        out_specs=vmem,
+        scratch_shapes=firsts
+        + recvs
+        + sends
+        + keeps
+        + [pltpu.VMEM(shape, kind) for shape, kind in buffers]
+        + [dma((3,)), dma((7,)), dma((7,)), dma, dma, dma((4,)), dma((4,)), dma((3,)), dma((3,)), dma((9, nb)), dma((9, nb))],
+        compiler_params=pltpu.CompilerParams(collective_id=0, has_side_effects=True, vmem_limit_bytes=63000000),
+    )(per_head_scale, tiles, grad_out, stem_weight, norm_gain[None], w_qkv, w_out, positions.reshape(-1, tok))
+
+
 def shards(patches, stem_weight, norm_gain, w_qkv, w_out, per_head_scale, positions, d_out):
     tiles = patches[0]
     grad_out = d_out[0]
+    chips = lax.axis_size("blk") * lax.axis_size("grid") // 2
+    if (grad_out.shape[1] // chips) % 16 == 0:
+        widths, parts = whole_layer(tiles, grad_out, stem_weight, norm_gain, w_qkv, w_out, per_head_scale, positions)
+        attn_end = sum(widths[:3])
+        qkv_end = sum(widths[:6])
+        stem_end = qkv_end + tiles.shape[1]
+        return (
+            parts[:, :, qkv_end:stem_end].transpose(0, 2, 1),
+            parts[0, :, stem_end] + parts[1, :, stem_end],
+            jnp.concatenate([parts[0, :, attn_end:qkv_end], parts[1, :, attn_end:qkv_end]], axis=1),
+            parts[:, :, :attn_end].transpose(0, 2, 1).reshape(2 * attn_end, -1),
+        )
     token_rows = tiles.shape[0]
     group_factor = QUERY_HEADS // KEY_VALUE_HEADS
     query_span_width = QUERY_HEADS * HEAD_SIZE
@@ -109,8 +489,6 @@
     attention_output = (
         jnp.stack(attn_list, axis=1).reshape(token_rows, query_span_width).astype(jnp.bfloat16)
     )
-    out_term = jnp.dot(attention_output.T, grad_out, preferred_element_type=jnp.float32)
-    d_w_out = lax.psum_scatter(out_term, ("blk", "grid"), scatter_dimension=1, tiled=True)
     dquery_list = []
     dkey_list = []
     dvalue_list = []
@@ -160,9 +538,9 @@
     dvalue_all = jnp.stack(dvalue_list, axis=1).reshape(every_key, key_span_width)
     partial_terms = jnp.concatenate([dkey_all, dvalue_all], axis=1)
     pieces = [partial_terms[offset * token_rows : (offset + 1) * token_rows] for offset in range(4)]
-    carried_state = pieces[3]
-    for offset in (2, 1, 0):
-        carried_state = passed_along(carried_state, "blk", -1) + pieces[offset]
+    carried_state = pieces[0]
+    for offset in (1, 2, 3):
+        carried_state = carried_state + passed_along(pieces[offset], "blk", -offset)
     pull_query = jax.vjp(head_norm, query)[1]
     gather_key = jax.vjp(head_norm, key)[1]
     dq_full = pull_query(query_gradient)[0].reshape(token_rows, query_span_width)
@@ -172,7 +550,6 @@
     d_qkv = jnp.concatenate(
         [dq_full, key_gradient_whole, carried_state[:, key_span_width:]], axis=1
     ).astype(jnp.bfloat16)
-    qkv_term = jnp.dot(hidden.T, d_qkv, preferred_element_type=jnp.float32)
     d_hidden = jnp.dot(d_qkv, w_qkv.T, preferred_element_type=jnp.float32)
     gain_term = jnp.sum(d_hidden * normed, axis=0)
     pull_tokens = jax.vjp(row_norm, token_f)[1]
@@ -185,11 +562,12 @@
             jnp.dot(below.T, d_tokens, preferred_element_type=jnp.float32),
         ]
     )
-    d_stem_weight, d_norm_gain, d_w_qkv = (
-        lax.psum_scatter(stem_term, ("blk", "grid"), scatter_dimension=2, tiled=True),
-        lax.psum_scatter(gain_term, ("blk", "grid"), scatter_dimension=0, tiled=True),
-        lax.psum_scatter(qkv_term, ("blk", "grid"), scatter_dimension=0, tiled=True),
-    )
+    qkv_term = jnp.dot(hidden.T, d_qkv, preferred_element_type=jnp.float32)
+    out_term = jnp.dot(attention_output.T, grad_out, preferred_element_type=jnp.float32)
+    d_stem_weight = lax.psum_scatter(stem_term, ("blk", "grid"), scatter_dimension=2, tiled=True)
+    d_norm_gain = lax.psum_scatter(gain_term, ("blk", "grid"), scatter_dimension=0, tiled=True)
+    d_w_qkv = lax.psum_scatter(qkv_term, ("blk", "grid"), scatter_dimension=0, tiled=True)
+    d_w_out = lax.psum_scatter(out_term, ("blk", "grid"), scatter_dimension=1, tiled=True)
     return (d_stem_weight, d_norm_gain, d_w_qkv, d_w_out)
 
 

time: 403 us -> 81.2 us (0.20)
  waiting for transfers between devices: 248 us -> 0 us
  Pallas kernels: 0 us -> 72.9 us
  matrix products: 44 us -> 0 us
  blocking collectives: 40.9 us -> 0 us
  starting transfers between devices: 16.9 us -> 0 us
  other arithmetic: 18.6 us -> 2.01 us
  between operations: 14.6 us -> 0.64 us
  local copies, waits for them, and re-layouts: 19.2 us -> 5.27 us
    reduce_scatter x3 -> x0, waiting for transfers between devices: 233 us -> none  [the longest x1 120 us: shards(): lax.psum_scatter(stem_term, ('blk', 'grid'), scatter_dimension=2, tiled=T...]
    pallas_call x0 -> x1, Pallas kernels: none -> 72.9 us  [whole_layer(): pl.pallas_call(partial(layer_kernel, (nb, grid_bits, orders, part_widths,...]
    unnamed x1 -> x0, blocking collectives: 40.9 us -> none
    dot_general x29 -> x0, matrix products: 34.8 us -> none  [the longest x4 5.45 us: shards(): jnp.einsum('trd,sd->rts', grad_group, value_cube[:, query_head_group], pr...]
    ppermute x7 -> x0, starting transfers between devices: 16.6 us -> none  [the longest x6 15.4 us: passed_along(): return lax.ppermute(x, axis, [(i, (i + by) % peers) for i in range(peers)])]
    ppermute x7 -> x0, waiting for transfers between devices: 14.1 us -> none  [the longest x6 14.1 us: passed_along(): return lax.ppermute(x, axis, [(i, (i + by) % peers) for i in range(peers)])]
    sub x4 -> x0, matrix products: 9.17 us -> none  [shards(): weights = jnp.where(visible, jnp.exp(attention_scores - top), 0.0)]
    slice x10 -> x0, local copies, waits for them, and re-layouts: 7.51 us -> none  [the longest x2 1.99 us: shards(): causal_window[:, key_span_width:]]
  transfers between devices with their start and end apart: 10 -> 0, of which waited for: 7 -> 0; matrix products, arithmetic and copies ran while one was open for 12% -> 0% of each run, Pallas kernels for 0% -> 0%
where the time goes in v2:
time: 81.2 us; the launch traced here: 80.8 us
  Pallas kernels  72.9 us (90%)
  local copies, waits for them, and re-layouts  5.27 us (6%)
  other arithmetic  2.01 us (2%)
    pallas_call x1, Pallas kernels, whole_layer(): pl.pallas_call(partial(layer_kernel, (nb, grid_bits, orders, part_widths,...  72.9 us

profile of v2, /device:TPU:0, one launch (start us, length us, event | category | flops | bytes accessed | tf_op | source)
XLA Modules:
  0.0 80.8 jit_solution(1667863362695938710)
XLA Ops:
  0.6 1.3 %broadcast_in_dim.3.refs_4_ = bf16[1,768]{1,0:T(2,128)(2,1)} reshape(bf16[768]{0:T(1024)(128)(2,1)} %param.10) | data formatting | bytes 3072 | tf_op jit(solution)/shard_map/broadcast_in_dim | solution.py:396
  1.9 72.9 %shard_map.111 = f32[2,24,2176]{2,1,0:T(8,128)} custom-call(f32[12]{0:T(128)} %refs_0_.1, bf16[128,1024]{1,0:T(8,128)(2,1)} %bitcast.13, bf16[128,768]{1,0:T(8,128)(2,1)} %bitcast.14, bf16[2,1024,768]{2,1,0:T(8,128)(2,1)} %refs_3_.1, bf16[1,768]{1,0:T(2,128)(2,1)} %broadcast_in_dim.3.refs_4_, bf16[768,1280]{1,0:T(8,128)(2,1)} %refs_5_.1, ...), custom_call_target="tpu_custom_call" | custom-call | tf_op jit(solution)/shard_map/pallas_call | solution.py:384
  74.8 1.4 %add_reduce_fusion = f32[24]{0:T(128)} fusion(f32[2,24,2176]{2,1,0:T(8,128)} %shard_map.111), kind=kLoop, calls=%fused_computation.5 | loop fusion | flops 24 | bytes 288 | tf_op jit(solution)/shard_map/add | solution.py:410
  76.1 0.9 %slice_bitcast_fusion.1 = f32[2,3,8,384]{3,2,1,0:T(8,128)S(1)} fusion(f32[2,24,2176]{2,1,0:T(8,128)} %shard_map.111), kind=kLoop, calls=%fused_computation.2 | loop fusion | bytes 147456
  77.0 0.6 copy.13
  77.7 0.9 %slice_bitcast_fusion.3 = (f32[24,640]{1,0:T(8,128)S(1)}, f32[24,640]{1,0:T(8,128)S(1)}) fusion(f32[2,24,2176]{2,1,0:T(8,128)} %shard_map.111), kind=kLoop, calls=%fused_computation.4 | loop fusion | bytes 245760 | tf_op jit(solution)/shard_map/squeeze | solution.py:411
  78.5 1.6 %slice_bitcast_fusion = f32[2,1024,24]{1,2,0:T(8,128)} fusion(f32[2,24,2176]{2,1,0:T(8,128)} %shard_map.111), kind=kLoop, calls=%fused_computation | loop fusion | bytes 393216 | tf_op jit(solution)/shard_map/transpose | solution.py:409
  80.1 0.7 pad_maximum_fusion

commit v3 on v2

--- a/solution.py
+++ b/solution.py
@@ -74,8 +74,8 @@
 
 def layer_kernel(plan, *refs):
     nb, grid_bits, orders, widths, offsets = plan
-    (scale_ref, tiles_ref, grad_ref, stem_hbm, gain_ref, wqkv_hbm, wout_hbm, pos_ref, result_ref) = refs[:9]
-    scratch = list(refs[9:])
+    (scale_ref, tiles_ref, grad_ref, stem_hbm, gain_ref, wqkv_hbm, wout_hbm, pos_ref, stem_out, gain_out, qkv_out, out_out) = refs[:12]
+    scratch = list(refs[12:])
     parts = len(widths)
     first = [scratch.pop(0) for _ in range(parts)]
     recv = [[scratch.pop(0) for _ in range(nb)] for _ in range(parts)]
@@ -86,7 +86,7 @@
      load_sem, pair_send, pair_got, halo_send, halo_got, kv_send, kv_got, dkv_send, dkv_got, send_sem, recv_sem) = scratch
     tok, width = grad_ref.shape
     halo = image.shape[0] - 2 * tok
-    span = kv.shape[2] // 2
+    span = kv.shape[0] * 128
     group = QUERY_HEADS // KEY_VALUE_HEADS
     own_blk = lax.axis_index("blk")
     own_grid = lax.axis_index("grid")
@@ -126,32 +126,26 @@
         return push(source, target, pair_send.at[which], pair_got.at[which], other_core)
 
     own_rows = pl.ds(pl.multiple_of(core * tok, tok), tok)
-    tiles_copy = pair(0, tiles_ref, image.at[own_rows])
     halo_copy = push(tiles_ref.at[:halo], image.at[2 * tok :], halo_send, halo_got, above)
-    grad_copy = pair(1, grad_ref, grad_pair.at[core])
-    image[own_rows] = tiles_ref[...]
-    grad_pair[core] = grad_ref[...]
 
     loads[0].wait()
     stem = plain_dot(tiles_ref[...], stem_w[0])
-    tiles_copy.wait()
     halo_copy.wait()
 
     @pl.when(own_grid == grid_count - 1)
     def _():
         image[2 * tok :] = jnp.zeros((halo, image.shape[1]), image.dtype)
 
-    below = image[pl.ds(pl.multiple_of(core * tok + halo, halo), tok)]
+    below = jnp.concatenate([tiles_ref[halo:], image[2 * tok :]], axis=0)
     stem = stem + plain_dot(below, stem_w[1])
     token_f = stem.astype(jnp.bfloat16).astype(jnp.float32)
     inv = lax.rsqrt(jnp.sum(token_f * token_f, axis=1, keepdims=True) / width + 1e-05)
     normed = token_f * inv
     normed_ref[...] = normed
     inv_ref[...] = jnp.broadcast_to(inv, inv_ref.shape)
-    gain_f = gain_ref[...].astype(jnp.float32)
+    gain_f = gain_ref[...].astype(jnp.float32).reshape(1, width)
     hidden = (normed * gain_f).astype(jnp.bfloat16)
     hidden_pair[core] = hidden
-    hidden_copy = pair(2, hidden_pair.at[core], hidden_pair.at[core])
     loads[1].wait()
     key_start = QUERY_HEADS * HEAD_SIZE
     value_start = key_start + span
@@ -161,12 +155,18 @@
         return scale, (x * scale).astype(jnp.bfloat16)
 
     keys = plain_dot(hidden, wqkv[:, key_start:])
-    for at in range(0, span, 128):
-        x = keys[:, at : at + 128]
-        heads_inv[:, key_start + at : key_start + at + 128], kv[0, :, at : at + 128] = normalize(x)
-    kv[0, :, span:] = keys[:, span:].astype(jnp.bfloat16)
+    kv_copies = []
+    for u in range(span // 128):
+        at = u * 128
+        heads_inv[:, key_start + at : key_start + at + 128], kv[u, 0, :, :128] = normalize(keys[:, at : at + 128])
+        kv[u, 0, :, 128:] = keys[:, span + at : span + at + 128].astype(jnp.bfloat16)
+        kv_copies.append([push(kv.at[u, 0], kv.at[u, j], kv_send.at[u, j], kv_got.at[u, j], along(j)) for j in (3, 2, 1)])
     qk_ref[:, key_start:] = keys[:, :span]
-    kv_copies = [push(kv.at[0], kv.at[j], kv_send.at[j], kv_got.at[j], along(j)) for j in (1, 2, 3)]
+    tiles_copy = pair(0, tiles_ref, image.at[own_rows])
+    grad_copy = pair(1, grad_ref, grad_pair.at[core])
+    hidden_copy = pair(2, hidden_pair.at[core], hidden_pair.at[core])
+    image[own_rows] = tiles_ref[...]
+    grad_pair[core] = grad_ref[...]
     queries = plain_dot(hidden, wqkv[:, :key_start])
     qk_ref[:, :key_start] = queries
     for at in range(0, key_start, 128):
@@ -181,14 +181,16 @@
         column = jnp.broadcast_to(key_pos, (tok, tok)).T
         seen.append(column <= query_pos)
     visible = jnp.concatenate([jnp.where(x, 1.0, 0.0) for x in seen], axis=0) > 0.5
-    for copy in kv_copies:
-        copy.wait()
-
+    dkv_copies = []
     for g in range(KEY_VALUE_HEADS):
-        lanes = slice(g * HEAD_SIZE, (g + 1) * HEAD_SIZE)
-        value_lanes = slice(span + g * HEAD_SIZE, span + (g + 1) * HEAD_SIZE)
-        keys_g = kv[:, :, lanes].reshape(4 * tok, HEAD_SIZE)
-        values_g = kv[:, :, value_lanes].reshape(4 * tok, HEAD_SIZE)
+        u, low_lane = g // 2, g % 2 * HEAD_SIZE
+        lanes = slice(low_lane, low_lane + HEAD_SIZE)
+        value_lanes = slice(128 + low_lane, 128 + low_lane + HEAD_SIZE)
+        if g % 2 == 0:
+            for copy in kv_copies[u]:
+                copy.wait()
+        keys_g = kv[u, :, :, lanes].reshape(4 * tok, HEAD_SIZE)
+        values_g = kv[u, :, :, value_lanes].reshape(4 * tok, HEAD_SIZE)
         heads = [slice((g * group + i) * HEAD_SIZE, (g * group + i + 1) * HEAD_SIZE) for i in range(group)]
         queries_g = jnp.concatenate([qn[:, h] for h in heads], axis=0)
         grads_g = jnp.concatenate([da[:, h] for h in heads], axis=0)
@@ -216,12 +218,14 @@
             dq[:, heads[i]] = dq_g[i * tok : (i + 1) * tok]
         dkeys = plain_dot(ds_g, queries_g).reshape(4, tok, HEAD_SIZE)
         dvalues = plain_dot(low_g, grads_g).reshape(4, tok, HEAD_SIZE)
-        dkv_own[:, lanes] = dkeys[0]
-        dkv_own[:, value_lanes] = dvalues[0]
+        dkv_own[u, :, lanes] = dkeys[0]
+        dkv_own[u, :, value_lanes] = dvalues[0]
         for j in (1, 2, 3):
-            dkv_out[j - 1, :, lanes] = dkeys[j].astype(jnp.bfloat16)
-            dkv_out[j - 1, :, value_lanes] = dvalues[j].astype(jnp.bfloat16)
-    dkv_copies = [push(dkv_out.at[j - 1], dkv_in.at[j - 1], dkv_send.at[j - 1], dkv_got.at[j - 1], along(-j)) for j in (3, 2, 1)]
+            dkv_out[u, j - 1, :, lanes] = dkeys[j].astype(jnp.bfloat16)
+            dkv_out[u, j - 1, :, value_lanes] = dvalues[j].astype(jnp.bfloat16)
+        if g % 2 == 1:
+            for j in (3, 2, 1):
+                dkv_copies.append(push(dkv_out.at[u, j - 1], dkv_in.at[u, j - 1], dkv_send.at[u, j - 1], dkv_got.at[u, j - 1], along(-j)))
     half_attn = attn.shape[1] // 2
     attn_copy = pair(3, attn.at[:, pl.ds(pl.multiple_of((1 - core) * half_attn, 128), half_attn)], attn_pair.at[core])
     attn_pair[core] = attn[:, pl.ds(pl.multiple_of(core * half_attn, 128), half_attn)]
@@ -234,6 +238,7 @@
     for at in range(0, key_start, 128):
         dqkv[:, at : at + 128] = pull(at, dq[:, at : at + 128])
 
+    finals = []
     copies = [None] * parts
     steps = [0] * parts
     done = [None] * parts
@@ -273,6 +278,8 @@
             half = value.shape[0] // 2
             final[0, :, offsets[part] : offsets[part] + widths[part]] = value[:half]
             final[1, :, offsets[part] : offsets[part] + widths[part]] = value[half:]
+            cols = slice(offsets[part], offsets[part] + widths[part])
+            finals.append(pair(6 + part, final.at[1 - core, :, cols], final_recv.at[:, cols]))
             return
         left_over.remove(order[step])
         place_next = 1 << left_over.index(order[step + 1])
@@ -293,15 +300,18 @@
 
     for copy in dkv_copies:
         copy.wait()
-    total_kv = dkv_own[...]
-    for j in range(3):
-        total_kv = total_kv + dkv_in[j].astype(jnp.float32)
-    for at in range(0, span, 128):
-        dqkv[:, key_start + at : key_start + at + 128] = pull(key_start + at, total_kv[:, at : at + 128])
-    dqkv[:, value_start:] = total_kv[:, span:].astype(jnp.bfloat16)
+    for u in range(span // 128):
+        total_kv = dkv_own[u]
+        for j in range(3):
+            total_kv = total_kv + dkv_in[u, j].astype(jnp.float32)
+        at = key_start + u * 128
+        dqkv[:, at : at + 128] = pull(at, total_kv[:, :128])
+        dqkv[:, at + span : at + span + 128] = total_kv[:, 128:].astype(jnp.bfloat16)
     half_qkv = dqkv.shape[1] // 2
     dqkv_copy = pair(4, dqkv.at[:, pl.ds(pl.multiple_of((1 - core) * half_qkv, 128), half_qkv)], dqkv_pair.at[core])
     dqkv_pair[core] = dqkv[:, pl.ds(pl.multiple_of(core * half_qkv, 128), half_qkv)]
+    for part in attn_parts:
+        advance(part)
     d_hidden = rowwise_dot(dqkv[...], wqkv[...])
     normed = normed_ref[...]
     flow = d_hidden * gain_f
@@ -314,15 +324,25 @@
     hidden_copy.wait()
     dqkv_copy.wait()
     begin(qkv_parts, hidden_pair[...], dqkv_pair[...].reshape(2 * tok, half_qkv))
+    for part in attn_parts:
+        advance(part)
     token_copy.wait()
+    tiles_copy.wait()
     begin(stem_parts, token_pair[...], image[pl.ds(pl.multiple_of(core * halo, halo), 2 * tok)], gain_tile)
     for _ in range(nb):
         for part in range(parts):
-            advance(part)
-    copy = pair(6, final.at[1 - core], final_recv)
-    result_ref[core] = final[core]
-    copy.wait()
-    result_ref[1 - core] = final_recv[...]
+            if steps[part] < nb:
+                advance(part)
+    for copy in finals:
+        copy.wait()
+    half_out, gain_at = out_out.shape[1] // 2, offsets[6] + stem_out.shape[2]
+    for source, value in ((core, final.at[core]), (1 - core, final_recv)):
+        out_out[:, pl.ds(pl.multiple_of(source * half_out, 128), half_out)] = value[:, : offsets[3]]
+        qkv_out[:, pl.ds(pl.multiple_of(source * half_qkv, 128), half_qkv)] = value[:, offsets[3] : offsets[6]]
+        stem_out[source] = value[:, offsets[6] : gain_at]
+    gain_sum = final[core, :, gain_at:] + final_recv[:, gain_at:]
+    square = jnp.concatenate([gain_sum, jnp.zeros((128 - gain_sum.shape[0], 128), jnp.float32)], axis=0).T
+    gain_out[...] = square[:1, : gain_out.shape[1]]
 
 
 def whole_layer(tiles, grad_out, stem_weight, norm_gain, w_qkv, w_out, per_head_scale, positions):
@@ -338,7 +358,9 @@
         piece = (amount // 3 + 127) // 128 * 128
         part_widths += [piece, piece, amount - 2 * piece]
     offsets = [sum(part_widths[:i]) for i in range(9)]
-    orders = halving_orders(grid_bits, blk_bits) * 3
+    grid_first, low = list(range(grid_bits)), list(range(grid_bits, nb))
+    turned = [low[i:] + low[:i] for i in (0, 1, 1)]
+    orders = [grid_first + rest for rest in turned] + halving_orders(grid_bits, blk_bits) * 2
     firsts, recvs, sends, keeps = [], [], [], []
     for order, w in zip(orders, part_widths):
         inner = 1 << order[0]
@@ -364,10 +386,10 @@
         ((2, tok, qd // 2), bf),
         ((2, tok, half_qkv), bf),
         ((2, tok, width), bf),
-        ((4, tok, 2 * span), bf),
-        ((3, tok, 2 * span), bf),
-        ((tok, 2 * span), f32),
-        ((3, tok, 2 * span), bf),
+        ((span // 128, 4, tok, 256), bf),
+        ((span // 128, 3, tok, 256), bf),
+        ((span // 128, tok, 256), f32),
+        ((span // 128, 3, tok, 256), bf),
         ((tok, width), f32),
         ((tok, 128), f32),
         ((tok, qd + span), f32),
@@ -379,21 +401,25 @@
         ((tok, w_qkv.shape[1]), bf),
     ]
     dma = pltpu.SemaphoreType.DMA
+    halves = span // 128
     vmem = pl.BlockSpec(memory_space=pltpu.VMEM)
     hbm = pl.BlockSpec(memory_space=pl.ANY)
-    return part_widths, pl.pallas_call(
+    return pl.pallas_call(
         partial(layer_kernel, (nb, grid_bits, orders, part_widths, offsets)),
-        out_shape=jax.ShapeDtypeStruct((2, rows // 2, total), f32),
+        out_shape=[
+            jax.ShapeDtypeStruct(shape, f32)
+            for shape in ((2, rows // 2, pin), (1, rows // 2), (rows // 2, w_qkv.shape[1]), (rows // 2, qd))
+        ],
         in_specs=[pl.BlockSpec(memory_space=pltpu.SMEM), vmem, vmem, hbm, vmem, hbm, hbm, vmem],
-        out_specs=vmem,
+        out_specs=[vmem] * 4,
         scratch_shapes=firsts
         + recvs
         + sends
         + keeps
         + [pltpu.VMEM(shape, kind) for shape, kind in buffers]
-        + [dma((3,)), dma((7,)), dma((7,)), dma, dma, dma((4,)), dma((4,)), dma((3,)), dma((3,)), dma((9, nb)), dma((9, nb))],
+        + [dma((3,)), dma((15,)), dma((15,)), dma, dma, dma((halves, 4)), dma((halves, 4)), dma((halves, 3)), dma((halves, 3)), dma((9, nb)), dma((9, nb))],
         compiler_params=pltpu.CompilerParams(collective_id=0, has_side_effects=True, vmem_limit_bytes=63000000),
-    )(per_head_scale, tiles, grad_out, stem_weight, norm_gain[None], w_qkv, w_out, positions.reshape(-1, tok))
+    )(per_head_scale, tiles, grad_out, stem_weight, norm_gain, w_qkv, w_out, positions.reshape(-1, tok))
 
 
 def shards(patches, stem_weight, norm_gain, w_qkv, w_out, per_head_scale, positions, d_out):
@@ -401,16 +427,10 @@
     grad_out = d_out[0]
     chips = lax.axis_size("blk") * lax.axis_size("grid") // 2
     if (grad_out.shape[1] // chips) % 16 == 0:
-        widths, parts = whole_layer(tiles, grad_out, stem_weight, norm_gain, w_qkv, w_out, per_head_scale, positions)
-        attn_end = sum(widths[:3])
-        qkv_end = sum(widths[:6])
-        stem_end = qkv_end + tiles.shape[1]
-        return (
-            parts[:, :, qkv_end:stem_end].transpose(0, 2, 1),
-            parts[0, :, stem_end] + parts[1, :, stem_end],
-            jnp.concatenate([parts[0, :, attn_end:qkv_end], parts[1, :, attn_end:qkv_end]], axis=1),
-            parts[:, :, :attn_end].transpose(0, 2, 1).reshape(2 * attn_end, -1),
-        )
+        d_stem, d_gain, d_qkv, d_out_t = whole_layer(
+            tiles, grad_out, stem_weight, norm_gain, w_qkv, w_out, per_head_scale, positions
+        )
+        return (d_stem.transpose(0, 2, 1), d_gain.reshape(-1), d_qkv, d_out_t.T)
     token_rows = tiles.shape[0]
     group_factor = QUERY_HEADS // KEY_VALUE_HEADS
     query_span_width = QUERY_HEADS * HEAD_SIZE

time: 81.2 us -> 81.7 us (level)
  other arithmetic: 2.01 us -> 0 us
  Pallas kernels: 72.9 us -> 74.9 us
    unnamed x1 -> x4, local copies, waits for them, and re-layouts: 0.89 us -> 5.89 us
    pallas_call x1, Pallas kernels: 72.9 us -> 74.9 us  [whole_layer(): pl.pallas_call(partial(layer_kernel, (nb, grid_bits, orders, part_widths,...]
    transpose x1 -> x0, local copies, waits for them, and re-layouts: 1.62 us -> none  [shards(): parts[:, :, qkv_end:stem_end].transpose(0, 2, 1)]
    add x1 -> x0, other arithmetic: 1.35 us -> none  [shards(): parts[0, :, stem_end] + parts[1, :, stem_end]]
    broadcast_in_dim x1 -> x0, local copies, waits for them, and re-layouts: 1.26 us -> none  [whole_layer(): norm_gain[None]]
    squeeze x1 -> x0, local copies, waits for them, and re-layouts: 0.87 us -> none  [shards(): parts[0, :, attn_end:qkv_end]]
where the time goes in v3:
time: 81.7 us; the launch traced here: 81.4 us
  Pallas kernels  74.9 us (92%)
  local copies, waits for them, and re-layouts  5.89 us (7%)
    pallas_call x1, Pallas kernels, whole_layer(): pl.pallas_call(partial(layer_kernel, (nb, grid_bits, orders, part_widths,...  74.9 us
    unnamed x4, local copies, waits for them, and re-layouts  5.89 us

profile of v3, /device:TPU:0, one launch (start us, length us, event | category | flops | bytes accessed | tf_op | source)
XLA Modules:
  0.0 81.4 jit_solution(13148586408281755721)
XLA Ops:
  0.6 74.9 %shard_map.111 = (f32[2,24,1024]{2,1,0:T(8,128)}, f32[1,24]{1,0:T(1,128)}, f32[24,1280]{1,0:T(8,128)}, f32[24,768]{1,0:T(8,128)}) custom-call(f32[12]{0:T(128)} %refs_0_.1, bf16[128,1024]{1,0:T(8,128)(2,1)} %bitcast.6, bf16[128,768]{1,0:T(8,128)(2,1)} %bitcast.7, bf16[2,1024,768]{2,1,0:T(8,128)(2,1)} %refs_3_.1, bf16[768]{0:T(1024)(128)(2,1)} %refs_4_.1, ...), custom_call_target="tpu_custom_call" | custom-call | tf_op jit(solution)/shard_map/pallas_call | solution.py:407
  75.5 1.6 %copy.16 = f32[2,1024,24]{1,2,0:T(8,128)} copy(f32[2,1024,24]{1,2,0:T(8,128)} %bitcast.8) | data formatting | bytes 393216
  77.2 1.2 %copy.17 = f32[24]{0:T(128)} copy(f32[24]{0:T(128)} %bitcast.11) | data formatting | bytes 192
  78.3 1.6 %copy.18 = f32[24,1280]{1,0:T(8,128)} copy(f32[24,1280]{1,0:T(8,128)} %get-tuple-element.18) | data formatting | bytes 245760
  79.9 1.5 %copy.19 = f32[768,24]{0,1:T(8,128)} copy(f32[768,24]{0,1:T(8,128)} %bitcast.9) | data formatting | bytes 147456

commit v4 on v3

--- a/solution.py
+++ b/solution.py
@@ -74,8 +74,8 @@
 
 def layer_kernel(plan, *refs):
     nb, grid_bits, orders, widths, offsets = plan
-    (scale_ref, tiles_ref, grad_ref, stem_hbm, gain_ref, wqkv_hbm, wout_hbm, pos_ref, stem_out, gain_out, qkv_out, out_out) = refs[:12]
-    scratch = list(refs[12:])
+    (scale_ref, tiles_ref, grad_ref, stem_hbm, gain_ref, wqkv_hbm, wout_hbm, pos_ref, result_ref) = refs[:9]
+    scratch = list(refs[9:])
     parts = len(widths)
     first = [scratch.pop(0) for _ in range(parts)]
     recv = [[scratch.pop(0) for _ in range(nb)] for _ in range(parts)]
@@ -310,8 +310,6 @@
     half_qkv = dqkv.shape[1] // 2
     dqkv_copy = pair(4, dqkv.at[:, pl.ds(pl.multiple_of((1 - core) * half_qkv, 128), half_qkv)], dqkv_pair.at[core])
     dqkv_pair[core] = dqkv[:, pl.ds(pl.multiple_of(core * half_qkv, 128), half_qkv)]
-    for part in attn_parts:
-        advance(part)
     d_hidden = rowwise_dot(dqkv[...], wqkv[...])
     normed = normed_ref[...]
     flow = d_hidden * gain_f
@@ -324,8 +322,6 @@
     hidden_copy.wait()
     dqkv_copy.wait()
     begin(qkv_parts, hidden_pair[...], dqkv_pair[...].reshape(2 * tok, half_qkv))
-    for part in attn_parts:
-        advance(part)
     token_copy.wait()
     tiles_copy.wait()
     begin(stem_parts, token_pair[...], image[pl.ds(pl.multiple_of(core * halo, halo), 2 * tok)], gain_tile)
@@ -335,12 +331,17 @@
                 advance(part)
     for copy in finals:
         copy.wait()
-    half_out, gain_at = out_out.shape[1] // 2, offsets[6] + stem_out.shape[2]
-    for source, value in ((core, final.at[core]), (1 - core, final_recv)):
-        out_out[:, pl.ds(pl.multiple_of(source * half_out, 128), half_out)] = value[:, : offsets[3]]
-        qkv_out[:, pl.ds(pl.multiple_of(source * half_qkv, 128), half_qkv)] = value[:, offsets[3] : offsets[6]]
-        stem_out[source] = value[:, offsets[6] : gain_at]
-    gain_sum = final[core, :, gain_at:] + final_recv[:, gain_at:]
+    result_ref[core] = final[core]
+    result_ref[1 - core] = final_recv[...]
+
+
+def unpack_kernel(offsets, result_ref, stem_out, gain_out, qkv_out, out_out):
+    half_out, half_qkv, gain_at = out_out.shape[1] // 2, qkv_out.shape[1] // 2, offsets[6] + stem_out.shape[2]
+    for source in range(2):
+        out_out[:, source * half_out : (source + 1) * half_out] = result_ref[source, :, : offsets[3]]
+        qkv_out[:, source * half_qkv : (source + 1) * half_qkv] = result_ref[source, :, offsets[3] : offsets[6]]
+        stem_out[source] = result_ref[source, :, offsets[6] : gain_at]
+    gain_sum = result_ref[0, :, gain_at:] + result_ref[1, :, gain_at:]
     square = jnp.concatenate([gain_sum, jnp.zeros((128 - gain_sum.shape[0], 128), jnp.float32)], axis=0).T
     gain_out[...] = square[:1, : gain_out.shape[1]]
 
@@ -360,7 +361,7 @@
     offsets = [sum(part_widths[:i]) for i in range(9)]
     grid_first, low = list(range(grid_bits)), list(range(grid_bits, nb))
     turned = [low[i:] + low[:i] for i in (0, 1, 1)]
-    orders = [grid_first + rest for rest in turned] + halving_orders(grid_bits, blk_bits) * 2
+    orders = halving_orders(grid_bits, blk_bits) * 3
     firsts, recvs, sends, keeps = [], [], [], []
     for order, w in zip(orders, part_widths):
         inner = 1 << order[0]
@@ -404,14 +405,11 @@
     halves = span // 128
     vmem = pl.BlockSpec(memory_space=pltpu.VMEM)
     hbm = pl.BlockSpec(memory_space=pl.ANY)
-    return pl.pallas_call(
+    result = pl.pallas_call(
         partial(layer_kernel, (nb, grid_bits, orders, part_widths, offsets)),
-        out_shape=[
-            jax.ShapeDtypeStruct(shape, f32)
-            for shape in ((2, rows // 2, pin), (1, rows // 2), (rows // 2, w_qkv.shape[1]), (rows // 2, qd))
-        ],
+        out_shape=jax.ShapeDtypeStruct((2, rows // 2, total), f32),
         in_specs=[pl.BlockSpec(memory_space=pltpu.SMEM), vmem, vmem, hbm, vmem, hbm, hbm, vmem],
-        out_specs=[vmem] * 4,
+        out_specs=vmem,
         scratch_shapes=firsts
         + recvs
         + sends
@@ -420,6 +418,15 @@
         + [dma((3,)), dma((15,)), dma((15,)), dma, dma, dma((halves, 4)), dma((halves, 4)), dma((halves, 3)), dma((halves, 3)), dma((9, nb)), dma((9, nb))],
         compiler_params=pltpu.CompilerParams(collective_id=0, has_side_effects=True, vmem_limit_bytes=63000000),
     )(per_head_scale, tiles, grad_out, stem_weight, norm_gain, w_qkv, w_out, positions.reshape(-1, tok))
+    return pl.pallas_call(
+        partial(unpack_kernel, offsets),
+        out_shape=[
+            jax.ShapeDtypeStruct(shape, f32)
+            for shape in ((2, rows // 2, pin), (1, rows // 2), (rows // 2, w_qkv.shape[1]), (rows // 2, qd))
+        ],
+        in_specs=[vmem],
+        out_specs=[vmem] * 4,
+    )(result)
 
 
 def shards(patches, stem_weight, norm_gain, w_qkv, w_out, per_head_scale, positions, d_out):

time: 81.7 us -> 73.2 us (0.90)
  local copies, waits for them, and re-layouts: 5.89 us -> 0 us
  Pallas kernels: 74.9 us -> 72.4 us
    unnamed x4 -> x0, local copies, waits for them, and re-layouts: 5.89 us -> none
    pallas_call x1, Pallas kernels: 74.9 us -> 70.6 us  [whole_layer(): pl.pallas_call(partial(layer_kernel, (nb, grid_bits, orders, part_widths,...]
    pallas_call x0 -> x1, Pallas kernels: none -> 1.76 us  [whole_layer(): pl.pallas_call(partial(unpack_kernel, offsets), out_shape=[jax.ShapeDtype...]
where the time goes in v4:
time: 73.2 us; the launch traced here: 73 us
  Pallas kernels  72.4 us (99%)
    pallas_call x1, Pallas kernels, whole_layer(): pl.pallas_call(partial(layer_kernel, (nb, grid_bits, orders, part_widths,...  70.6 us
    pallas_call x1, Pallas kernels, whole_layer(): pl.pallas_call(partial(unpack_kernel, offsets), out_shape=[jax.ShapeDtype...  1.76 us

profile of v4, /device:TPU:0, one launch (start us, length us, event | category | flops | bytes accessed | tf_op | source)
XLA Modules:
  0.0 73.0 jit_solution(13892469987569341233)
XLA Ops:
  0.6 70.6 %shard_map.111.result_ref = f32[2,24,2176]{2,1,0:T(8,128)} custom-call(f32[12]{0:T(128)} %refs_0_.1, bf16[128,1024]{1,0:T(8,128)(2,1)} %bitcast.6, bf16[128,768]{1,0:T(8,128)(2,1)} %bitcast.7, bf16[2,1024,768]{2,1,0:T(8,128)(2,1)} %refs_3_.1, bf16[768]{0:T(1024)(128)(2,1)} %refs_4_.1, bf16[768,1280]{1,0:T(8,128)(2,1)} %refs_5_.1, bf16[768,768]{1,0:T(8,128)(2,1)} %refs_6_.1, ...), custom_call_target="tpu_custom_call" | custom-call | tf_op jit(solution)/shard_map/pallas_call | solution.py:408
  71.2 1.8 %shard_map.112 = (f32[2,24,1024]{2,1,0:T(8,128)}, f32[1,24]{1,0:T(1,128)}, f32[24,1280]{1,0:T(8,128)}, f32[24,768]{1,0:T(8,128)}) custom-call(f32[2,24,2176]{2,1,0:T(8,128)} %shard_map.111.result_ref), custom_call_target="tpu_custom_call" | custom-call | tf_op jit(solution)/shard_map/pallas_call | solution.py:421
